TPU v7x, 32 devices: a whole 2x2x4 slice. The times are simulated.
32 devices in a mesh: slab: 16 (over z, y, x), sect: 2 (over core).
Axes of the slice: x: 2, y: 2, z: 4, core: 2. Of those that a mesh axis runs over, the one named last changes fastest.
Arguments:
- fields: float32 [2, 2, 2048, 2048], P(None, None, 'slab'), may hold values from -6 to 6
- region_ids: int32 [2, 2048, 2048], P('sect', 'slab'), may hold values from 0 to 15
- index_offsets: float32 [2, 16], replicated, may hold values from -0.002 to 0.002
- step_lengths: float32 [2], replicated, may hold values from 500 to 2000
- wave_numbers: float32 [2], replicated, may hold values from 0.5 to 2
- zone_ids: int32 [2048, 2048], P('slab'), may hold values from 0 to 31
- zone_phases: float32 [2, 32], replicated, may hold values from -3.140625 to 3.140625
Outputs:
- propagated: float32 [2, 2, 2048, 2048], P('sect', None, 'slab')
All inputs are finite; a program needn't handle non-finite values.
Results may differ from a plain program's by a relative error of at most 0.00023.
Values sent between devices are 32-bit elements; how exact they have to be, the bound alone decides.
No kernel may reach another device: no remote copies, remote signals or barrier semaphores. Data moves between devices by JAX's collectives and lax.ppermute only.
A program may use at most 64 MiB of HBM per device.

v0:
```python
import math

import jax
import jax.numpy as jnp
from jax import lax
from jax.sharding import PartitionSpec as P

N1 = 16
N2 = 128
STEPS = 2


HIGHEST = lax.Precision.HIGHEST


def make_tables(first_len, second_len):
    total_len = first_len * second_len
    first_index = jnp.arange(first_len, dtype=jnp.int32)
    second_index = jnp.arange(second_len, dtype=jnp.int32)
    first_angle = (first_index[:, None] * first_index[None, :] % first_len).astype(jnp.float32) * (
        2.0 * math.pi / first_len
    )
    twist_angle = (first_index[:, None] * second_index[None, :]).astype(jnp.float32) * (
        2.0 * math.pi / total_len
    )
    second_angle = (second_index[:, None] * second_index[None, :] % second_len).astype(
        jnp.float32
    ) * (2.0 * math.pi / second_len)
    position = jnp.arange(total_len, dtype=jnp.int32)
    frequency = position // second_len + first_len * (position % second_len)
    spread = jnp.sin(frequency.astype(jnp.float32) * (math.pi / total_len)) ** 2
    return (
        jnp.cos(first_angle),
        jnp.sin(first_angle),
        jnp.cos(twist_angle),
        jnp.sin(twist_angle),
        jnp.cos(second_angle),
        jnp.sin(second_angle),
        spread,
    )


def left_apply(matrix, values):
    return jnp.einsum("kn,...nm->...km", matrix, values, precision=HIGHEST)


def right_apply(values, matrix):
    return jnp.einsum("...kn,nm->...km", values, matrix, precision=HIGHEST)


def forward(real_part, imaginary_part, tables):
    cos_one, sin_one, cos_twist, sin_twist, cos_two, sin_two = tables[:6]
    full_shape = real_part.shape
    grid_shape = full_shape[:-1] + (cos_one.shape[0], cos_two.shape[0])
    grid_real = real_part.reshape(grid_shape)
    grid_imaginary = imaginary_part.reshape(grid_shape)
    mixed_real = left_apply(cos_one, grid_real) + left_apply(sin_one, grid_imaginary)
    mixed_imaginary = left_apply(cos_one, grid_imaginary) - left_apply(sin_one, grid_real)
    turned_real = mixed_real * cos_twist + mixed_imaginary * sin_twist
    turned_imaginary = mixed_imaginary * cos_twist - mixed_real * sin_twist
    spectrum_real = right_apply(turned_real, cos_two) + right_apply(turned_imaginary, sin_two)
    spectrum_imaginary = right_apply(turned_imaginary, cos_two) - right_apply(turned_real, sin_two)
    return (spectrum_real.reshape(full_shape), spectrum_imaginary.reshape(full_shape))


def backward(real_part, imaginary_part, tables):
    cos_one, sin_one, cos_twist, sin_twist, cos_two, sin_two = tables[:6]
    full_shape = real_part.shape
    grid_shape = full_shape[:-1] + (cos_one.shape[0], cos_two.shape[0])
    inverse_count = 1.0 / (cos_one.shape[0] * cos_two.shape[0])
    grid_real = real_part.reshape(grid_shape)
    grid_imaginary = imaginary_part.reshape(grid_shape)
    turned_real = right_apply(grid_real, cos_two) - right_apply(grid_imaginary, sin_two)
    turned_imaginary = right_apply(grid_imaginary, cos_two) + right_apply(grid_real, sin_two)
    mixed_real = turned_real * cos_twist - turned_imaginary * sin_twist
    mixed_imaginary = turned_imaginary * cos_twist + turned_real * sin_twist
    plain_real = left_apply(cos_one, mixed_real) - left_apply(sin_one, mixed_imaginary)
    plain_imaginary = left_apply(cos_one, mixed_imaginary) + left_apply(sin_one, mixed_real)
    return (
        (plain_real * inverse_count).reshape(full_shape),
        (plain_imaginary * inverse_count).reshape(full_shape),
    )


def crank_factor(wave_number, length, spread):
    curvature = -4.0 * spread[None, :] / (wave_number[:, None] * wave_number[:, None])
    stiffness = wave_number[:, None] * length * 0.25
    front_part = 1.0 + 0.25 * curvature
    cross_part = stiffness * curvature
    magnitude = front_part * front_part + cross_part * cross_part
    factor_real = (front_part * front_part - cross_part * cross_part) / magnitude
    factor_imaginary = 2.0 * front_part * cross_part / magnitude
    return (factor_real[:, None, :], factor_imaginary[:, None, :])


def half_step(real_part, imaginary_part, factor_real, factor_imaginary, tables):
    spectrum_real, spectrum_imaginary = forward(real_part, imaginary_part, tables)
    scaled_real = spectrum_real * factor_real - spectrum_imaginary * factor_imaginary
    scaled_imaginary = spectrum_real * factor_imaginary + spectrum_imaginary * factor_real
    return backward(scaled_real, scaled_imaginary, tables)


def apply_screen(real_part, imaginary_part, phase):
    cosine = jnp.cos(phase)
    sine_value = jnp.sin(phase)
    return (
        real_part * cosine - imaginary_part * sine_value,
        real_part * sine_value + imaginary_part * cosine,
    )


def pick_values(labels, table):
    picked = jnp.zeros(table.shape[:-1] + labels.shape[-2:], jnp.float32)
    for entry in range(table.shape[-1]):
        picked = picked + jnp.where(labels == entry, table[..., entry][..., None, None], 0.0)
    return picked


def pack_blocks(block, peers):
    leading = block.shape[:-2]
    row_count = block.shape[-2]
    column_count = block.shape[-1] // peers
    lead_count = len(leading)
    shaped = block.reshape(leading + (row_count, peers, column_count))
    permute = tuple(range(lead_count)) + (lead_count + 1, lead_count + 2, lead_count)
    return jnp.transpose(shaped, permute).reshape(leading + (peers, column_count * row_count))


def unpack_blocks(block, peers, row_count):
    leading = block.shape[:-2]
    column_count = block.shape[-1] // row_count
    lead_count = len(leading)
    shaped = block.reshape(leading + (peers, column_count, row_count))
    permute = tuple(range(lead_count)) + (lead_count + 1, lead_count, lead_count + 2)
    return jnp.transpose(shaped, permute).reshape(leading + (column_count, peers * row_count))


def flip_fields(state):
    peers = lax.axis_size("slab")
    moved = lax.all_to_all(
        pack_blocks(state, peers), "slab", split_axis=2, concat_axis=2, tiled=True
    )
    return unpack_blocks(moved, peers, state.shape[-2])


def flip_parts(real_part, imaginary_part):
    turned = flip_fields(jnp.stack([real_part, imaginary_part], axis=1))
    return (turned[:, 0], turned[:, 1])


def propagate(state, wave_number, lens, iol_flags, row_offsets, lengths, tables):
    spread = tables[6]
    real_part = state[:, 0]
    imaginary_part = state[:, 1]
    for section in range(row_offsets.shape[0]):
        length = lengths[section]
        factor_real, factor_imaginary = crank_factor(wave_number, length, spread)
        entrance = jnp.where(iol_flags[section], lens, 0.0)
        for step_index in range(STEPS):
            phase = wave_number[:, None, None] * length * row_offsets[section][None]
            if step_index == 0:
                phase = phase + entrance
            real_part, imaginary_part = apply_screen(real_part, imaginary_part, phase)
            real_part, imaginary_part = half_step(
                real_part, imaginary_part, factor_real, factor_imaginary, tables
            )
            real_part, imaginary_part = flip_parts(real_part, imaginary_part)
            real_part, imaginary_part = half_step(
                real_part, imaginary_part, factor_real, factor_imaginary, tables
            )
            real_part, imaginary_part = flip_parts(real_part, imaginary_part)
    return jnp.stack([real_part, imaginary_part], axis=1)


def shards(fields, region_ids, index_offsets, step_lengths, wave_numbers, zone_ids, zone_phases):
    tables = make_tables(N1, N2)
    segment_index = lax.axis_index("sect")
    segments = lax.axis_size("sect")
    local_count = region_ids.shape[0]
    field_count = fields.shape[0]
    half_count = field_count // segments
    last_section = local_count * segments - 1
    local_table = lax.dynamic_slice_in_dim(
        index_offsets, segment_index * local_count, local_count, 0
    )
    offsets = pick_values(region_ids, local_table)
    sections = lax.all_gather(offsets, "sect", axis=0, tiled=True)
    iol_flags = [position == last_section for position in range(local_count * segments)]
    mine = lax.dynamic_slice_in_dim(fields, segment_index * half_count, half_count, 0)
    numbers = lax.dynamic_slice_in_dim(wave_numbers, segment_index * half_count, half_count, 0)
    phases_mine = lax.dynamic_slice_in_dim(zone_phases, segment_index * half_count, half_count, 0)
    lens_mine = pick_values(zone_ids, phases_mine)
    return propagate(mine, numbers, lens_mine, iol_flags, sections, step_lengths, tables)


def solution(mesh):
    return jax.shard_map(
        shards,
        mesh=mesh,
        in_specs=(
            P(None, None, "slab", None),
            P("sect", "slab", None),
            P(),
            P(),
            P(),
            P("slab", None),
            P(),
        ),
        out_specs=P("sect", None, "slab", None),
        check_vma=False,
    )
```

profile of v0, /device:TPU:0, one launch (start us, length us, event | category | flops | bytes accessed | tf_op | source)
XLA Modules:
  0.0 762.1 jit_solution(3803213570587671836)
XLA Ops:
  8.0 13.8 %select_add_fusion = f32[1,128,2048]{2,1,0:T(8,128)} fusion(s32[1,128,2048]{2,1,0:T(8,128)} %param.8, f32[]{:T(128)} %bitcast.17, f32[]{:T(128)} %bitcast.16, f32[]{:T(128)} %bitcast.15, f32[]{:T(128)} %bitcast.14, f32[]{:T(128)} %bitcast.13, f32[]{:T(128)} %bitcast.12, f32[]{:T(128)} %bitcast.11, f32[]{:T(128)} %bitcast.10, f32[]{:T(128)} %bitcast.9, ...), kind=kLoop, calls=%fused_computation.187 | loop fusion | flops 12320768 | bytes 2097216 | tf_op jit(solution)/shard_map/add | solution.py:115
  28.2 7.0 all-gather.2.cloned.1.call-done
  35.2 3.1 fusion.984
  39.9 4.9 fusion.49
  44.8 1.7 copy.301
  46.5 2.0 fusion.385
  71.9 1.9 copy.312
  75.5 55.8 %all_to_all.40 = f32[1,2,16,16384]{3,0,1,2:T(1,128)S(1)} all-to-all(f32[1,2,16,16384]{3,0,1,2:T(1,128)S(1)} %copy.313), channel_id=1, replica_groups=mesh['slab'=16,'sect'=2] {'slab'}, dimensions={2} | all-to-all | bytes 4194304 | tf_op jit(solution)/shard_map/all_to_all | solution.py:140
  132.8 1.9 copy.315
  137.9 2.0 fusion.379
  163.3 1.9 copy.326
  166.9 52.0 %all_to_all.41 = f32[1,2,16,16384]{3,0,1,2:T(1,128)S(1)} all-to-all(f32[1,2,16,16384]{3,0,1,2:T(1,128)S(1)} %copy.327), channel_id=1, replica_groups=mesh['slab'=16,'sect'=2] {'slab'}, dimensions={2} | all-to-all | bytes 4194304 | tf_op jit(solution)/shard_map/all_to_all | solution.py:140
  220.4 1.9 copy.329
  222.3 4.9 multiply_add_fusion.14
  227.2 1.7 copy.331
  230.0 1.7 copy.330
  253.3 1.9 copy.342
  256.9 51.8 %all_to_all.42 = f32[1,2,16,16384]{3,0,1,2:T(1,128)S(1)} all-to-all(f32[1,2,16,16384]{3,0,1,2:T(1,128)S(1)} %copy.343), channel_id=1, replica_groups=mesh['slab'=16,'sect'=2] {'slab'}, dimensions={2} | all-to-all | bytes 4194304 | tf_op jit(solution)/shard_map/all_to_all | solution.py:140
  310.1 2.1 copy.345
  314.9 1.7 copy.456
  338.1 1.9 copy.356
  340.0 3.2 copy.357
  343.2 4.6 all-to-all-start.3
  351.3 27.8 %fusion.979 = (f32[1,128,2048]{1,2,0:T(8,128)}, f32[1,128,2048]{1,2,0:T(8,128)}) fusion(f32[]{:T(128)} %bitcast.144, s32[128,2048]{0,1:T(8,128)S(1)} %copy.361, f32[]{:T(128)} %bitcast.143, f32[]{:T(128)} %bitcast.142, f32[]{:T(128)} %bitcast.141, f32[]{:T(128)} %bitcast.140, f32[]{:T(128)} %bitcast.139, f32[]{:T(128)} %bitcast.138, f32[]{:T(128)} %bitcast.137, ...), kind=kLoop, calls=%fused_computation.1014 | loop fusion | flops 25427968 | bytes 4194436 | tf_op jit(solution)/shard_map/cos | solution.py:104
  379.1 10.4 %all-to-all-done.3 = f32[1,2,16,16384]{3,0,1,2:T(1,128)} async-done(((f32[1,2,16,16384]{3,0,1,2:T(1,128)}), f32[1,2,16,16384]{3,0,1,2:T(1,128)}, u32[]{:S(2)}, u32[]{:S(2)}) %all-to-all-start.3) | async-done | bytes 2097184 | tf_op jit(solution)/shard_map/all_to_all | solution.py:140
  389.6 3.1 copy.358
  392.7 1.9 copy.359
  394.6 5.8 multiply_add_fusion.9
  400.5 1.7 copy.394
  402.2 2.0 fusion.361
  427.7 1.9 copy.405
  431.3 57.7 %all_to_all.43 = f32[1,2,16,16384]{3,0,1,2:T(1,128)S(1)} all-to-all(f32[1,2,16,16384]{3,0,1,2:T(1,128)S(1)} %copy.406), channel_id=1, replica_groups=mesh['slab'=16,'sect'=2] {'slab'}, dimensions={2} | all-to-all | bytes 4194304 | tf_op jit(solution)/shard_map/all_to_all | solution.py:140
  490.4 1.9 copy.408
  495.5 2.0 fusion.355
  521.0 1.9 copy.419
  524.6 51.7 %all_to_all.44 = f32[1,2,16,16384]{3,0,1,2:T(1,128)S(1)} all-to-all(f32[1,2,16,16384]{3,0,1,2:T(1,128)S(1)} %copy.420), channel_id=1, replica_groups=mesh['slab'=16,'sect'=2] {'slab'}, dimensions={2} | all-to-all | bytes 4194304 | tf_op jit(solution)/shard_map/all_to_all | solution.py:140
  577.7 1.9 copy.422
  579.6 4.9 multiply_add_fusion.4
  584.5 1.7 copy.424
  587.3 1.7 copy.423
  610.5 1.9 copy.435
  614.2 51.5 %all_to_all.45 = f32[1,2,16,16384]{3,0,1,2:T(1,128)S(1)} all-to-all(f32[1,2,16,16384]{3,0,1,2:T(1,128)S(1)} %copy.436), channel_id=1, replica_groups=mesh['slab'=16,'sect'=2] {'slab'}, dimensions={2} | all-to-all | bytes 4194304 | tf_op jit(solution)/shard_map/all_to_all | solution.py:140
  667.1 2.1 copy.438
  671.9 1.7 copy.460
  695.0 1.9 copy.449
  698.6 51.5 %all_to_all.46 = f32[1,2,16,16384]{3,0,1,2:T(1,128)S(1)} all-to-all(f32[1,2,16,16384]{3,0,1,2:T(1,128)S(1)} %copy.450), channel_id=1, replica_groups=mesh['slab'=16,'sect'=2] {'slab'}, dimensions={2} | all-to-all | bytes 4194304 | tf_op jit(solution)/shard_map/all_to_all | solution.py:140
  750.2 1.8 copy.452
  752.1 2.9 copy.453
  (196 shorter events, 222.1 us)
Async XLA Ops:
  6.5 342.9 %copy-start = (f32[2,32]{1,0:T(2,128)S(1)}, f32[2,32]{1,0:T(2,128)}, u32[]{:S(2)}) copy-start(f32[2,32]{1,0:T(2,128)} %param.13) | copy-start | bytes 772
  6.5 15.2 %copy-start.9 = (f32[2]{0:T(128)S(1)}, f32[2]{0:T(128)}, u32[]{:S(2)}) copy-start(f32[2]{0:T(128)} %param.11) | copy-start | bytes 28
  6.5 17.3 %copy-start.8 = (f32[2]{0:T(128)S(1)}, f32[2]{0:T(128)}, u32[]{:S(2)}) copy-start(f32[2]{0:T(128)} %param.10) | copy-start | bytes 28
  6.5 28.7 %all-gather.2.cloned.1.call-start = ((), (), s32[]{:S(2)}) async-start(), calls=%async_computation.8 | async-start | bytes 3145728 | tf_op jit(solution)/shard_map/all_gather | solution.py:187
  50.3 1.2 copy-start.2
  141.7 1.2 copy-start.3
  343.2 5.9 copy-start.7
  343.2 46.4 %all-to-all-start.3 = ((f32[1,2,16,16384]{3,0,1,2:T(1,128)}), f32[1,2,16,16384]{3,0,1,2:T(1,128)}, u32[]{:S(2)}, u32[]{:S(2)}) async-start(f32[1,2,16,16384]{3,0,1,2:T(1,128)} %copy.357), calls=%async_computation.3 | async-start | bytes 4194304 | tf_op jit(solution)/shard_map/all_to_all | solution.py:140
  347.7 3.2 copy-start.6
  406.0 1.2 copy-start.4
  499.3 1.2 copy-start.5
  752.1 2.9 copy-start.1
Sparse Core Ops, SparseCore 0:
  21.9 13.2 all-gather.1
where the time goes:
time: 768 us; the launch traced here: 762 us
  blocking collectives  372 us (48%)
  matrix products  182 us (24%)
  local copies, waits for them, and re-layouts  104 us (14%)
  other arithmetic  63.4 us (8%)
  between operations  19.1 us (2%)
  waiting for transfers between devices  17.5 us (2%)
    all_to_all x7, blocking collectives, flip_fields(): lax.all_to_all(pack_blocks(state, peers), 'slab', split_axis=2, concat_ax...  372 us
    dot_general x64, matrix products, left_apply(): return jnp.einsum('kn,...nm->...km', matrix, values, precision=HIGHEST)  92.1 us
    dot_general x64, matrix products, right_apply(): return jnp.einsum('...kn,nm->...km', values, matrix, precision=HIGHEST)  89.9 us
    cos x1, other arithmetic, apply_screen(): cosine = jnp.cos(phase)  27.8 us
    another operation x16, local copies, waits for them, and re-layouts  25.2 us
    add x4, other arithmetic, apply_screen(): real_part * sine_value + imaginary_part * cosine  20.5 us
    transpose x8, local copies, waits for them, and re-layouts, unpack_blocks(): jnp.transpose(shaped, permute)  15.6 us
  transfers between devices with their start and end apart: 2, of which 2 were waited for; matrix products, arithmetic and copies ran while one was open for 4% of the time, Pallas kernels for 0%

commit v1 on v0

v1 whole, which is shorter than its diff:
```python
import math
import jax
import jax.numpy as jnp
from jax import lax
from jax.sharding import PartitionSpec as P

STEPS = 2
BLOCK = 128
HIGHEST = lax.Precision.HIGHEST


def c_mul(a, b):
    return a[0] * b[0] - a[1] * b[1], a[0] * b[1] + a[1] * b[0]


def c_add(a, b):
    return a[0] + b[0], a[1] + b[1]


def c_div(a, b):
    size = b[0] * b[0] + b[1] * b[1]
    return (a[0] * b[0] + a[1] * b[1]) / size, (a[1] * b[0] - a[0] * b[1]) / size


def c_sqrt(a):
    size = jnp.sqrt(a[0] * a[0] + a[1] * a[1])
    real = jnp.sqrt(0.5 * (size + a[0]))
    return real, 0.5 * a[1] / real


def c_power(theta, count):
    size = jnp.exp(-theta[0] * count)
    angle = theta[1] * count
    return size * jnp.cos(angle), -size * jnp.sin(angle)


def scalars(number, length):
    sigma = number * length * 0.25
    size = 0.0625 + sigma * sigma
    square = number * number / size
    z = (-0.0625 * square, -0.25 * sigma * square)
    sinh = c_sqrt(z)
    cosh = c_sqrt((1.0 + z[0], z[1]))
    small = c_add(sinh, c_div(z, (1.0 + cosh[0], cosh[1])))
    theta = (
        jnp.log1p(2.0 * small[0] + small[0] * small[0] + small[1] * small[1]),
        2.0 * jnp.arctan2(small[1], 1.0 + small[0]),
    )
    front = (-2.0 * sigma * sigma / size, -0.5 * sigma / size)
    gamma = c_mul(front, c_div(sinh, cosh))
    alpha = ((0.0625 - sigma * sigma) / size, 0.5 * sigma / size)
    return theta, gamma, c_mul(alpha, alpha)


def closure(theta, total):
    power = c_power(theta, float(total))
    return c_div((jnp.ones_like(power[0]), jnp.zeros_like(power[0])), (1.0 - power[0], -power[1]))


def toeplitz(theta, gamma, count):
    index = jnp.arange(count, dtype=jnp.int32)
    apart = jnp.abs(index[:, None] - index[None, :])
    real, imaginary = c_mul(gamma, c_power(theta, apart.astype(jnp.float32)))
    return jnp.where(apart == 0, 1.0, 0.0) + real, imaginary


def circulant(theta, size, blocks):
    index = jnp.arange(blocks, dtype=jnp.int32)
    apart = jnp.mod(index[:, None] - index[None, :] - 1, blocks).astype(jnp.float32)
    return c_mul(closure(theta, size * blocks), c_power(theta, apart * size))


def c_ein(spec, a, b):
    def one(x, y):
        return jnp.einsum(spec, x, y, precision=HIGHEST)

    return one(a[0], b[0]) - one(a[1], b[1]), one(a[0], b[1]) + one(a[1], b[0])


def spans(theta, gamma, count):
    index = jnp.arange(count, dtype=jnp.int32).astype(jnp.float32)
    weight_left = c_mul(gamma, c_power(theta, count - 1 - index))
    weight_right = c_mul(gamma, c_power(theta, index))
    reach_left = c_power(theta, index + 1)
    reach_right = c_power(theta, count - index)
    return weight_left, weight_right, reach_left, reach_right


def row_solve(x, theta, gamma):
    shape = x[0].shape
    blocks = shape[-1] // BLOCK
    x = tuple(part.reshape(shape[:-1] + (blocks, BLOCK)) for part in x)
    weight_left, weight_right, reach_left, reach_right = spans(theta, gamma, BLOCK)
    ring = circulant(theta, BLOCK, blocks)
    y = c_ein("...bi,ij->...bj", x, toeplitz(theta, gamma, BLOCK))
    left = c_ein("...b,cb->...c", c_ein("...bi,i->...b", x, weight_left), ring)
    right = c_ein("...b,bc->...c", c_ein("...bi,i->...b", x, weight_right), ring)
    y = c_add(y, c_ein("...b,i->...bi", left, reach_left))
    y = c_add(y, c_ein("...b,i->...bi", right, reach_right))
    return tuple(part.reshape(shape) for part in y)


def pick_values(labels, table):
    picked = jnp.zeros(labels.shape, jnp.float32)
    for entry in range(table.shape[-1]):
        picked = picked + jnp.where(labels == entry, table[entry], 0.0)
    return picked


def column_local(x, theta, gamma, rows):
    weight_left, weight_right, _, _ = spans(theta, gamma, rows)
    y = c_ein("ij,jm->im", toeplitz(theta, gamma, rows), x)
    return y, c_ein("i,im->m", weight_left, x), c_ein("i,im->m", weight_right, x)


def reach(y, left, right, theta, gamma, rows):
    _, _, reach_left, reach_right = spans(theta, gamma, rows)
    y = c_add(y, c_ein("i,m->im", reach_left, left))
    return c_add(y, c_ein("i,m->im", reach_right, right))


def payload(y, left, right, screen, theta, gamma, rows):
    weight_left, weight_right, reach_left, reach_right = spans(theta, gamma, rows)
    z = c_mul(screen, y)
    parts = [left, right, c_ein("i,im->m", weight_left, z), c_ein("i,im->m", weight_right, z)]
    for weight, other in ((weight_left, reach_left), (weight_left, reach_right), (weight_right, reach_left)):
        parts.append(c_ein("i,im->m", c_mul(weight, other), screen))
    return jnp.stack([half for part in parts for half in part])


def exchange(packed, theta, rows):
    peers = lax.axis_size("slab")
    width = packed.shape[-1] // peers
    sent = jnp.swapaxes(packed.reshape(packed.shape[0], peers, width), 0, 1)
    held = lax.all_to_all(sent, "slab", 0, 0, tiled=True)
    one = [(held[:, 2 * i], held[:, 2 * i + 1]) for i in range(7)]
    ring = circulant(theta, rows, peers)
    left = c_ein("cb,bm->cm", ring, one[0])
    right = c_ein("bc,bm->cm", ring, one[1])
    next_left = c_add(one[2], c_add(c_mul(one[4], left), c_mul(one[5], right)))
    next_right = c_add(one[3], c_add(c_mul(one[6], left), c_mul(one[4], right)))
    next_left = c_ein("cb,bm->cm", ring, next_left)
    next_right = c_ein("bc,bm->cm", ring, next_right)
    back = jnp.stack([half for part in (left, right, next_left, next_right) for half in part], axis=1)
    back = lax.all_to_all(back, "slab", 0, 0, tiled=True)
    back = jnp.swapaxes(back, 0, 1).reshape(8, peers * width)
    return [(back[2 * i], back[2 * i + 1]) for i in range(4)]


def shards(fields, region_ids, index_offsets, step_lengths, wave_numbers, zone_ids, zone_phases):
    mine = lax.axis_index("sect")
    other = lax.ppermute(region_ids, "sect", [(0, 1), (1, 0)])
    labels = [jnp.where(mine == s, region_ids[0], other[0]) for s in range(2)]
    field = lax.dynamic_index_in_dim(fields, mine, 0, False)
    number = lax.dynamic_index_in_dim(wave_numbers, mine, 0, False)
    phases = lax.dynamic_index_in_dim(zone_phases, mine, 0, False)
    rows = field.shape[1]
    u = (field[0], field[1])
    lens = (pick_values(zone_ids, jnp.cos(phases)), pick_values(zone_ids, jnp.sin(phases)))
    for section in range(2):
        theta, gamma, turn = scalars(number, step_lengths[section])
        phase = number * step_lengths[section] * index_offsets[section]
        table = c_mul(turn, (jnp.cos(phase), jnp.sin(phase)))
        screen = tuple(pick_values(labels[section], half) for half in table)
        u = c_mul(u, screen)
        if section == 1:
            u = c_mul(u, lens)
        u, left, right = column_local(row_solve(u, theta, gamma), theta, gamma, rows)
        sent = payload(u, left, right, screen, theta, gamma, rows)
        back = exchange(sent, theta, rows)
        u = reach(u, back[0], back[1], theta, gamma, rows)
        u, _, _ = column_local(row_solve(c_mul(u, screen), theta, gamma), theta, gamma, rows)
        left = row_solve(back[2], theta, gamma)
        right = row_solve(back[3], theta, gamma)
        u = reach(u, left, right, theta, gamma, rows)
    return jnp.stack(u)[None]


def solution(mesh):
    return jax.shard_map(
        shards,
        mesh=mesh,
        in_specs=(
            P(None, None, "slab", None),
            P("sect", "slab", None),
            P(),
            P(),
            P(),
            P("slab", None),
            P(),
        ),
        out_specs=P("sect", None, "slab", None),
        check_vma=False,
    )
```

time: 768 us -> 532 us (0.69)
  blocking collectives: 372 us -> 22.1 us
  matrix products: 182 us -> 326 us
  local copies, waits for them, and re-layouts: 104 us -> 22.2 us
  other arithmetic: 63.4 us -> 125 us
  between operations: 19.1 us -> 8.57 us
  waiting for transfers between devices: 17.5 us -> 8.34 us
    all_to_all x7 -> x2, blocking collectives: 372 us -> 22.1 us  [the longest x1 11.9 us: exchange(): held = lax.all_to_all(sent, 'slab', 0, 0, tiled=True)]
    dot_general x128 -> x264, matrix products: 182 us -> 326 us  [one(): return jnp.einsum(spec, x, y, precision=HIGHEST)]
    add x5 -> x27, other arithmetic: 34.3 us -> 106 us  [the longest x9 82.3 us: c_mul(): return (a[0] * b[0] - a[1] * b[1], a[0] * b[1] + a[1] * b[0])]
    transpose x16 -> x0, local copies, waits for them, and re-layouts: 30.6 us -> none  [the longest x8 15.6 us: unpack_blocks(): jnp.transpose(shaped, permute)]
    cos x1 -> x0, other arithmetic: 27.8 us -> none  [apply_screen(): cosine = jnp.cos(phase)]
    another operation x16 -> x4, local copies, waits for them, and re-layouts: 25.2 us -> 2.32 us  [the longest x2 1.61 us: payload(): return jnp.stack([half for part in parts for half in part])]
    reshape x9 -> x0, local copies, waits for them, and re-layouts: 18.1 us -> none  [the longest x8 15.2 us: pack_blocks(): jnp.transpose(shaped, permute)]
    eq x0 -> x3, other arithmetic: none -> 13.9 us  [pick_values(): picked = picked + jnp.where(labels == entry, table[entry], 0.0)]
  transfers between devices with their start and end apart: 2 -> 3, of which waited for: 2 -> 2; matrix products, arithmetic and copies ran while one was open for 4% -> 6% of each run, Pallas kernels for 0% -> 0%
where the time goes in v1:
time: 532 us; the launch traced here: 525 us
  matrix products  326 us (61%)
  other arithmetic  125 us (23%)
  local copies, waits for them, and re-layouts  22.2 us (4%)
  blocking collectives  22.1 us (4%)
  starting transfers between devices  11.8 us (2%)
  between operations  8.57 us (2%)
  waiting for transfers between devices  8.34 us (2%)
    dot_general x264, matrix products, one(): return jnp.einsum(spec, x, y, precision=HIGHEST)  326 us
    add x9, other arithmetic, c_mul(): return (a[0] * b[0] - a[1] * b[1], a[0] * b[1] + a[1] * b[0])  82.3 us
    add x2, other arithmetic, pick_values(): picked = picked + jnp.where(labels == entry, table[entry], 0.0)  23.4 us
    eq x3, other arithmetic, pick_values(): picked = picked + jnp.where(labels == entry, table[entry], 0.0)  13.9 us
    all_to_all x1, blocking collectives, exchange(): held = lax.all_to_all(sent, 'slab', 0, 0, tiled=True)  11.9 us
  transfers between devices with their start and end apart: 3, of which 2 were waited for; matrix products, arithmetic and copies ran while one was open for 6% of the time, Pallas kernels for 0%

profile of v1, /device:TPU:0, one launch (start us, length us, event | category | flops | bytes accessed | tf_op | source)
XLA Modules:
  0.0 524.7 jit_solution(15068183581703305335)
XLA Ops:
  14.8 1.7 dynamic-slice_bitcast_fusion.1
  23.3 6.7 %broadcast_compare_fusion.31 = (pred[128,2048]{1,0:T(8,128)(4,1)}, pred[128,2048]{1,0:T(8,128)(4,1)}, pred[128,2048]{1,0:T(8,128)(4,1)}, pred[128,2048]{1,0:T(8,...) fusion(s32[128,2048]{1,0:T(8,128)S(1)} %copy-done.52), kind=kLoop, calls=%fused_computation.340 | loop fusion | flops 8388608 | bytes 9437184 | tf_op jit(solution)/shard_map/eq | solution.py:106
  31.0 12.7 %add_add_fusion.1 = (f32[1,128,2048]{2,1,0:T(8,128)S(1)}, pred[1,128,2048]{2,1,0:T(8,128)(4,1)S(1)}, pred[1,128,2048]{2,1,0:T(8,128)(4,1)S(1)}, pred[1,128,2048]...) fusion(f32[]{:T(128)} %bitcast.16, f32[]{:T(128)} %bitcast.15, ...), kind=kLoop, calls=%fused_computation.276 | loop fusion | flops 11272192 | bytes 7077948 | tf_op jit(solution)/shard_map/add | solution.py:106
  43.8 10.7 %add_add_fusion = f32[1,128,2048]{2,1,0:T(8,128)S(1)} fusion(pred[1,128,2048]{2,1,0:T(8,128)(4,1)S(1)} %get-tuple-element.50, pred[1,128,2048]{2,1,0:T(8,128)(4,1)S(1)} %get-tuple-element.49, pred[1,128,2048]{2,1,0:T(8,128)(4,1)S(1)} %get-tuple-element.48, pred[1,128,2048]{2,1,0:T(8,128)(4,1)S(1)} %get-tuple-element.47, ...), kind=kLoop, calls=%fused_computation.275 | loop fusion | flops 7077888 | bytes 4718648 | tf_op jit(solution)/shard_map/add | solution.py:106
  57.9 2.2 multiply_add_fusion.6
  71.5 2.7 fusion.543
  74.1 2.2 fusion.541
  76.4 2.2 fusion.549
  81.3 2.3 fusion.158
  88.0 2.4 fusion.18
  96.3 4.3 multiply_add_fusion.5
  122.8 7.9 %all-to-all-start = ((f32[16,14,128]{2,1,0:T(8,128)}), f32[16,14,128]{2,1,0:T(8,128)S(1)}, u32[]{:S(2)}, u32[]{:S(2)}) async-start(f32[16,14,128]{2,1,0:T(8,128)} %bitcast.131), calls=%async_computation | async-start | bytes 262144 | tf_op jit(solution)/shard_map/all_to_all | solution.py:135
  130.6 2.5 broadcast_compare_fusion.62
  133.1 5.6 %all-to-all-done = f32[16,14,128]{2,1,0:T(8,128)S(1)} async-done(((f32[16,14,128]{2,1,0:T(8,128)}), f32[16,14,128]{2,1,0:T(8,128)S(1)}, u32[]{:S(2)}, u32[]{:S(2)}) %all-to-all-start) | async-done | bytes 114720 | tf_op jit(solution)/shard_map/all_to_all | solution.py:135
  143.2 3.5 all-to-all-start.1
  146.7 4.8 broadcast_compare_fusion.60
  151.5 2.7 all-to-all-done.1
  154.3 2.1 multiply_add_fusion.4
  156.6 7.4 %fusion.555 = f32[1,128,16]{2,0,1:T(1,128)S(1)} fusion(f32[128,16,128]{2,1,0:T(8,128)S(1)} %bitcast.1541, f32[128]{0:T(128)S(1)} %get-tuple-element.27), kind=kOutput, calls=%fused_computation.829 | convolution fusion | flops 3145728 | bytes 1057280 | tf_op jit(solution)/shard_map/...bi,i->...b/dot_general | solution.py:75
  164.0 7.4 %fusion.561 = f32[1,128,16]{2,0,1:T(1,128)S(1)} fusion(f32[128,16,128]{2,1,0:T(8,128)S(1)} %bitcast.1542, f32[128]{0:T(128)S(1)} %get-tuple-element.26), kind=kOutput, calls=%fused_computation.835 | convolution fusion | flops 3145728 | bytes 1057280 | tf_op jit(solution)/shard_map/...bi,i->...b/dot_general | solution.py:75
  172.9 7.5 %fusion.563 = f32[1,128,16]{2,0,1:T(1,128)S(1)} fusion(f32[128,16,128]{2,1,0:T(8,128)S(1)} %bitcast.1553, f32[128]{0:T(128)S(1)} %get-tuple-element.26), kind=kOutput, calls=%fused_computation.837 | convolution fusion | flops 3145728 | bytes 1057280 | tf_op jit(solution)/shard_map/...bi,i->...b/dot_general | solution.py:75
  180.5 7.4 %fusion.553 = f32[1,128,16]{2,0,1:T(1,128)S(1)} fusion(f32[128,16,128]{2,1,0:T(8,128)S(1)} %bitcast.1554, f32[128]{0:T(128)S(1)} %get-tuple-element.27), kind=kOutput, calls=%fused_computation.827 | convolution fusion | flops 3145728 | bytes 1057280 | tf_op jit(solution)/shard_map/...bi,i->...b/dot_general | solution.py:75
  188.4 7.4 %fusion.539 = f32[1,128,16]{2,0,1:T(1,128)S(1)} fusion(f32[128,16,128]{2,1,0:T(8,128)S(1)} %bitcast.1543, f32[128]{0:T(128)S(1)} %copy-done.62), kind=kOutput, calls=%fused_computation.813 | convolution fusion | flops 3145728 | bytes 1057280 | tf_op jit(solution)/shard_map/...bi,i->...b/dot_general | solution.py:75
  195.8 7.6 %fusion.547 = f32[1,128,16]{2,0,1:T(1,128)S(1)} fusion(f32[128,16,128]{2,1,0:T(8,128)S(1)} %bitcast.1555, f32[128]{0:T(128)S(1)} %copy-done.59), kind=kOutput, calls=%fused_computation.821 | convolution fusion | flops 3145728 | bytes 1057280 | tf_op jit(solution)/shard_map/...bi,i->...b/dot_general | solution.py:75
  203.4 7.4 %fusion.545 = f32[1,128,16]{2,0,1:T(1,128)S(1)} fusion(f32[128,16,128]{2,1,0:T(8,128)S(1)} %bitcast.1544, f32[128]{0:T(128)S(1)} %copy-done.59), kind=kOutput, calls=%fused_computation.819 | convolution fusion | flops 3145728 | bytes 1057280 | tf_op jit(solution)/shard_map/...bi,i->...b/dot_general | solution.py:75
  210.8 7.4 %fusion.537 = f32[1,128,16]{2,0,1:T(1,128)S(1)} fusion(f32[128,16,128]{2,1,0:T(8,128)S(1)} %bitcast.1556, f32[128]{0:T(128)S(1)} %copy-done.62), kind=kOutput, calls=%fused_computation.811 | convolution fusion | flops 3145728 | bytes 1057280 | tf_op jit(solution)/shard_map/...bi,i->...b/dot_general | solution.py:75
  226.5 2.1 fusion.20
  241.0 73.7 %multiply_add_fusion.2 = (f32[128,2048]{1,0:T(8,128)S(1)}, f32[128,2048]{1,0:T(8,128)S(1)}, f32[128,2048]{1,0:T(8,128)S(1)}, f32[128,2048]{1,0:T(8,128)S(1)}, f3...) fusion(pred[128,2048]{1,0:T(8,128)(4,1)S(1)} %copy-done.42, f32[]{:T(128)} %bitcast.326, ...), kind=kLoop, calls=%fused_computation.283 | loop fusion | flops 51642368 | bytes 22020480 | tf_op jit(solution)/shard_map/add | solution.py:13
  324.0 7.4 %fusion.463 = f32[1,128,16]{2,0,1:T(1,128)S(1)} fusion(f32[128,16,128]{2,1,0:T(8,128)S(1)} %bitcast.1545, f32[128]{0:T(128)S(1)} %get-tuple-element.12), kind=kOutput, calls=%fused_computation.737 | convolution fusion | flops 3145728 | bytes 1057280 | tf_op jit(solution)/shard_map/...bi,i->...b/dot_general | solution.py:75
  331.4 7.8 %fusion.453 = f32[1,128,16]{2,0,1:T(1,128)S(1)} fusion(f32[128,16,128]{2,1,0:T(8,128)S(1)} %bitcast.1546, f32[128]{0:T(128)S(1)} %get-tuple-element.11), kind=kOutput, calls=%fused_computation.727 | convolution fusion | flops 3145728 | bytes 1057280 | tf_op jit(solution)/shard_map/...bi,i->...b/dot_general | solution.py:75
  339.4 7.4 %fusion.455 = f32[1,128,16]{2,0,1:T(1,128)S(1)} fusion(f32[128,16,128]{2,1,0:T(8,128)S(1)} %bitcast.1557, f32[128]{0:T(128)S(1)} %get-tuple-element.11), kind=kOutput, calls=%fused_computation.729 | convolution fusion | flops 3145728 | bytes 1057280 | tf_op jit(solution)/shard_map/...bi,i->...b/dot_general | solution.py:75
  346.8 7.4 %fusion.461 = f32[1,128,16]{2,0,1:T(1,128)S(1)} fusion(f32[128,16,128]{2,1,0:T(8,128)S(1)} %bitcast.1558, f32[128]{0:T(128)S(1)} %get-tuple-element.12), kind=kOutput, calls=%fused_computation.735 | convolution fusion | flops 3145728 | bytes 1057280 | tf_op jit(solution)/shard_map/...bi,i->...b/dot_general | solution.py:75
  354.7 7.6 %fusion.447 = f32[1,128,16]{2,0,1:T(1,128)S(1)} fusion(f32[128,16,128]{2,1,0:T(8,128)S(1)} %bitcast.1547, f32[128]{0:T(128)S(1)} %copy-done.54), kind=kOutput, calls=%fused_computation.721 | convolution fusion | flops 3145728 | bytes 1057280 | tf_op jit(solution)/shard_map/...bi,i->...b/dot_general | solution.py:75
  362.3 7.4 %fusion.439 = f32[1,128,16]{2,0,1:T(1,128)S(1)} fusion(f32[128,16,128]{2,1,0:T(8,128)S(1)} %bitcast.1559, f32[128]{0:T(128)S(1)} %copy-done.56), kind=kOutput, calls=%fused_computation.713 | convolution fusion | flops 3145728 | bytes 1057280 | tf_op jit(solution)/shard_map/...bi,i->...b/dot_general | solution.py:75
  369.7 7.4 %fusion.437 = f32[1,128,16]{2,0,1:T(1,128)S(1)} fusion(f32[128,16,128]{2,1,0:T(8,128)S(1)} %bitcast.1548, f32[128]{0:T(128)S(1)} %copy-done.56), kind=kOutput, calls=%fused_computation.711 | convolution fusion | flops 3145728 | bytes 1057280 | tf_op jit(solution)/shard_map/...bi,i->...b/dot_general | solution.py:75
  377.1 7.4 %fusion.445 = f32[1,128,16]{2,0,1:T(1,128)S(1)} fusion(f32[128,16,128]{2,1,0:T(8,128)S(1)} %bitcast.1560, f32[128]{0:T(128)S(1)} %copy-done.54), kind=kOutput, calls=%fused_computation.719 | convolution fusion | flops 3145728 | bytes 1057280 | tf_op jit(solution)/shard_map/...bi,i->...b/dot_general | solution.py:75
  396.6 2.8 multiply_add_fusion.1
  412.4 11.9 %all_to_all.20 = f32[16,14,128]{2,1,0:T(8,128)S(1)} all-to-all(f32[16,14,128]{2,1,0:T(8,128)S(1)} %bitcast.1637), channel_id=1, replica_groups=mesh['slab'=16,'sect'=2] {'slab'}, dimensions={0} | all-to-all | bytes 229376 | tf_op jit(solution)/shard_map/all_to_all | solution.py:135
  428.1 10.2 %all_to_all.21 = f32[16,8,128]{2,1,0:T(8,128)S(1)} all-to-all(f32[16,8,128]{2,1,0:T(8,128)S(1)} %copy.69), channel_id=1, replica_groups=mesh['slab'=16,'sect'=2] {'slab'}, dimensions={0} | all-to-all | bytes 131072 | tf_op jit(solution)/shard_map/all_to_all | solution.py:145
  439.5 7.4 %fusion.459 = f32[1,128,16]{2,0,1:T(1,128)S(1)} fusion(f32[128,16,128]{2,1,0:T(8,128)S(1)} %bitcast.1549, f32[128]{0:T(128)S(1)} %get-tuple-element.12), kind=kOutput, calls=%fused_computation.733 | convolution fusion | flops 3145728 | bytes 1057280 | tf_op jit(solution)/shard_map/...bi,i->...b/dot_general | solution.py:75
  446.8 7.4 %fusion.449 = f32[1,128,16]{2,0,1:T(1,128)S(1)} fusion(f32[128,16,128]{2,1,0:T(8,128)S(1)} %bitcast.1550, f32[128]{0:T(128)S(1)} %get-tuple-element.11), kind=kOutput, calls=%fused_computation.723 | convolution fusion | flops 3145728 | bytes 1057280 | tf_op jit(solution)/shard_map/...bi,i->...b/dot_general | solution.py:75
  454.4 7.6 %fusion.451 = f32[1,128,16]{2,0,1:T(1,128)S(1)} fusion(f32[128,16,128]{2,1,0:T(8,128)S(1)} %bitcast.1561, f32[128]{0:T(128)S(1)} %get-tuple-element.11), kind=kOutput, calls=%fused_computation.725 | convolution fusion | flops 3145728 | bytes 1057280 | tf_op jit(solution)/shard_map/...bi,i->...b/dot_general | solution.py:75
  462.0 7.4 %fusion.457 = f32[1,128,16]{2,0,1:T(1,128)S(1)} fusion(f32[128,16,128]{2,1,0:T(8,128)S(1)} %bitcast.1562, f32[128]{0:T(128)S(1)} %get-tuple-element.12), kind=kOutput, calls=%fused_computation.731 | convolution fusion | flops 3145728 | bytes 1057280 | tf_op jit(solution)/shard_map/...bi,i->...b/dot_general | solution.py:75
  469.9 7.4 %fusion.443 = f32[1,128,16]{2,0,1:T(1,128)S(1)} fusion(f32[128,16,128]{2,1,0:T(8,128)S(1)} %bitcast.1551, f32[128]{0:T(128)S(1)} %copy-done.54), kind=kOutput, calls=%fused_computation.717 | convolution fusion | flops 3145728 | bytes 1057280 | tf_op jit(solution)/shard_map/...bi,i->...b/dot_general | solution.py:75
  477.3 7.4 %fusion.435 = f32[1,128,16]{2,0,1:T(1,128)S(1)} fusion(f32[128,16,128]{2,1,0:T(8,128)S(1)} %bitcast.1563, f32[128]{0:T(128)S(1)} %copy-done.56), kind=kOutput, calls=%fused_computation.709 | convolution fusion | flops 3145728 | bytes 1057280 | tf_op jit(solution)/shard_map/...bi,i->...b/dot_general | solution.py:75
  484.7 7.6 %fusion.433 = f32[1,128,16]{2,0,1:T(1,128)S(1)} fusion(f32[128,16,128]{2,1,0:T(8,128)S(1)} %bitcast.1552, f32[128]{0:T(128)S(1)} %copy-done.56), kind=kOutput, calls=%fused_computation.707 | convolution fusion | flops 3145728 | bytes 1057280 | tf_op jit(solution)/shard_map/...bi,i->...b/dot_general | solution.py:75
  492.3 7.4 %fusion.441 = f32[1,128,16]{2,0,1:T(1,128)S(1)} fusion(f32[128,16,128]{2,1,0:T(8,128)S(1)} %bitcast.1564, f32[128]{0:T(128)S(1)} %copy-done.54), kind=kOutput, calls=%fused_computation.715 | convolution fusion | flops 3145728 | bytes 1057280 | tf_op jit(solution)/shard_map/...bi,i->...b/dot_general | solution.py:75
  509.3 1.9 fusion.24
  (494 shorter events, 155.5 us)
Async XLA Ops:
  0.0 30.0 %collective-permute-start = (s32[1,128,2048]{2,1,0:T(8,128)}, s32[1,128,2048]{2,1,0:T(8,128)S(1)}, u32[]{:S(2)}, u32[]{:S(2)}) collective-permute-start(s32[1,128,2048]{2,1,0:T(8,128)} %param.8), channel_id=1, source_target_pairs={{0,1},{1,0},{2,3},{3,2},{4,5},{5,4},{6,7},{7,6},{8,9},{9,8},{10,11... | collective-permute-start | bytes 3145736 | tf_op jit(solution)/shard_map/ppermute | solution.py:152
  16.5 6.8 %copy-start.52 = (s32[128,2048]{1,0:T(8,128)S(1)}, s32[128,2048]{1,0:T(8,128)}, u32[]{:S(2)}) copy-start(s32[128,2048]{1,0:T(8,128)} %param.12) | copy-start | bytes 3145732
  21.4 8.6 %copy-start.57 = (f32[128]{0:T(128)}, f32[128]{0:T(128)S(1)}, u32[]{:S(2)}) copy-start(f32[128]{0:T(128)S(1)} %get-tuple-element.23) | copy-start | bytes 1540
  21.4 8.6 %copy-start.60 = (f32[128]{0:T(128)}, f32[128]{0:T(128)S(1)}, u32[]{:S(2)}) copy-start(f32[128]{0:T(128)S(1)} %get-tuple-element.24) | copy-start | bytes 1540
  21.4 8.6 %copy-start.67 = (f32[128]{0:T(128)}, f32[128]{0:T(128)S(1)}, u32[]{:S(2)}) copy-start(f32[128]{0:T(128)S(1)} %get-tuple-element.21) | copy-start | bytes 1540
  21.4 8.6 %copy-start.70 = (f32[128]{0:T(128)}, f32[128]{0:T(128)S(1)}, u32[]{:S(2)}) copy-start(f32[128]{0:T(128)S(1)} %get-tuple-element.22) | copy-start | bytes 1540
  22.0 8.0 %copy-start.53 = (f32[128]{0:T(128)}, f32[128]{0:T(128)S(1)}, u32[]{:S(2)}) copy-start(f32[128]{0:T(128)S(1)} %get-tuple-element.9) | copy-start | bytes 1540
  22.0 8.0 %copy-start.55 = (f32[128]{0:T(128)}, f32[128]{0:T(128)S(1)}, u32[]{:S(2)}) copy-start(f32[128]{0:T(128)S(1)} %get-tuple-element.8) | copy-start | bytes 1540
  22.0 8.0 %copy-start.63 = (f32[128]{0:T(128)}, f32[128]{0:T(128)S(1)}, u32[]{:S(2)}) copy-start(f32[128]{0:T(128)S(1)} %get-tuple-element.6) | copy-start | bytes 1540
  22.0 8.0 %copy-start.65 = (f32[128]{0:T(128)}, f32[128]{0:T(128)S(1)}, u32[]{:S(2)}) copy-start(f32[128]{0:T(128)S(1)} %get-tuple-element.7) | copy-start | bytes 1540
  23.3 6.8 %copy-start.5 = (s32[1,128,2048]{2,1,0:T(8,128)S(1)}, s32[1,128,2048]{2,1,0:T(8,128)}, u32[]{:S(2)}) copy-start(s32[1,128,2048]{2,1,0:T(8,128)} %param.8) | copy-start | bytes 3145732
  43.8 10.9 %copy-start.10 = (pred[1,128,2048]{2,1,0:T(32,128)(4,1)}, pred[1,128,2048]{2,1,0:T(32,128)(4,1)S(1)}, u32[]{:S(2)}) copy-start(pred[1,128,2048]{2,1,0:T(32,128)(4,1)S(1)} %get-tuple-element.79) | copy-start | bytes 786436
  43.8 11.8 %copy-start.1 = (f32[1,128,2048]{2,1,0:T(8,128)}, f32[1,128,2048]{2,1,0:T(8,128)S(1)}, u32[]{:S(2)}) copy-start(f32[1,128,2048]{2,1,0:T(8,128)S(1)} %get-tuple-element.36) | copy-start | bytes 3145732
  81.3 5.8 %copy-start.79 = (f32[1,128,16]{1,0,2:T(1,128)S(1)}, f32[1,128,16]{1,0,2:T(1,128)}, u32[]{:S(2)}) copy-start(f32[1,128,16]{1,0,2:T(1,128)} %fusion.541) | copy-start | bytes 24580
  81.3 5.9 %copy-start.78 = (f32[1,128,16]{1,0,2:T(1,128)S(1)}, f32[1,128,16]{1,0,2:T(1,128)}, u32[]{:S(2)}) copy-start(f32[1,128,16]{1,0,2:T(1,128)} %fusion.549) | copy-start | bytes 24580
  81.3 6.0 %copy-start.81 = (f32[128,16]{0,1:T(8,128)S(1)}, f32[128,16]{0,1:T(8,128)}, u32[]{:S(2)}) copy-start(f32[128,16]{0,1:T(8,128)} %fusion.186) | copy-start | bytes 24580
  81.3 6.3 %copy-start.80 = (f32[128,16]{0,1:T(8,128)S(1)}, f32[128,16]{0,1:T(8,128)}, u32[]{:S(2)}) copy-start(f32[128,16]{0,1:T(8,128)} %fusion.185) | copy-start | bytes 24580
  87.9 3.8 copy-start.8
  87.9 3.8 copy-start.68
  96.3 4.3 copy-start.85
  100.6 8.6 %copy-start = (f32[128,2048]{1,0:T(8,128)}, f32[128,2048]{1,0:T(8,128)S(1)}, u32[]{:S(2)}) copy-start(f32[128,2048]{1,0:T(8,128)S(1)} %get-tuple-element.306) | copy-start | bytes 3145732
  122.8 16.0 %all-to-all-start = ((f32[16,14,128]{2,1,0:T(8,128)}), f32[16,14,128]{2,1,0:T(8,128)S(1)}, u32[]{:S(2)}, u32[]{:S(2)}) async-start(f32[16,14,128]{2,1,0:T(8,128)} %bitcast.131), calls=%async_computation | async-start | bytes 262144 | tf_op jit(solution)/shard_map/all_to_all | solution.py:135
  143.2 11.0 %all-to-all-start.1 = ((f32[16,8,128]{2,1,0:T(8,128)}), f32[16,8,128]{2,1,0:T(8,128)S(1)}, u32[]{:S(2)}, u32[]{:S(2)}) async-start(f32[16,8,128]{2,1,0:T(8,128)} %copy.50), calls=%async_computation.1 | async-start | bytes 131072 | tf_op jit(solution)/shard_map/all_to_all | solution.py:145
  146.7 7.6 %copy-start.69 = (f32[128]{0:T(128)S(1)}, f32[128]{0:T(128)}, u32[]{:S(2)}) copy-start(f32[128]{0:T(128)} %copy-done.67) | copy-start | bytes 1540
  146.7 7.6 %copy-start.72 = (f32[128]{0:T(128)S(1)}, f32[128]{0:T(128)}, u32[]{:S(2)}) copy-start(f32[128]{0:T(128)} %copy-done.70) | copy-start | bytes 1540
  146.7 7.6 %copy-start.75 = (f32[128]{0:T(128)S(1)}, f32[128]{0:T(128)}, u32[]{:S(2)}) copy-start(f32[128]{0:T(128)} %get-tuple-element.324) | copy-start | bytes 1540
  146.7 7.6 %copy-start.77 = (f32[128]{0:T(128)S(1)}, f32[128]{0:T(128)}, u32[]{:S(2)}) copy-start(f32[128]{0:T(128)} %get-tuple-element.325) | copy-start | bytes 1540
  172.7 15.7 %copy-start.62 = (f32[128]{0:T(128)S(1)}, f32[128]{0:T(128)}, u32[]{:S(2)}) copy-start(f32[128]{0:T(128)} %copy-done.60) | copy-start | bytes 1540
  172.9 22.9 %copy-start.59 = (f32[128]{0:T(128)S(1)}, f32[128]{0:T(128)}, u32[]{:S(2)}) copy-start(f32[128]{0:T(128)} %copy-done.57) | copy-start | bytes 1540
  234.0 6.6 %copy-start.46 = (pred[1,128,2048]{2,1,0:T(8,128)(4,1)S(1)}, pred[1,128,2048]{2,1,0:T(8,128)(4,1)}, u32[]{:S(2)}) copy-start(pred[1,128,2048]{2,1,0:T(8,128)(4,1)} %get-tuple-element.65) | copy-start | bytes 786436
  234.1 6.6 %copy-start.47 = (pred[1,128,2048]{2,1,0:T(8,128)(4,1)S(1)}, pred[1,128,2048]{2,1,0:T(8,128)(4,1)}, u32[]{:S(2)}) copy-start(pred[1,128,2048]{2,1,0:T(8,128)(4,1)} %get-tuple-element.66) | copy-start | bytes 786436
  234.1 6.6 %copy-start.48 = (pred[1,128,2048]{2,1,0:T(8,128)(4,1)S(1)}, pred[1,128,2048]{2,1,0:T(8,128)(4,1)}, u32[]{:S(2)}) copy-start(pred[1,128,2048]{2,1,0:T(8,128)(4,1)} %get-tuple-element.67) | copy-start | bytes 786436
  234.1 6.6 %copy-start.49 = (pred[1,128,2048]{2,1,0:T(8,128)(4,1)S(1)}, pred[1,128,2048]{2,1,0:T(8,128)(4,1)}, u32[]{:S(2)}) copy-start(pred[1,128,2048]{2,1,0:T(8,128)(4,1)} %get-tuple-element.68) | copy-start | bytes 786436
  234.1 6.6 %copy-start.50 = (pred[1,128,2048]{2,1,0:T(8,128)(4,1)S(1)}, pred[1,128,2048]{2,1,0:T(8,128)(4,1)}, u32[]{:S(2)}) copy-start(pred[1,128,2048]{2,1,0:T(8,128)(4,1)} %get-tuple-element.69) | copy-start | bytes 786436
  234.1 6.6 %copy-start.51 = (pred[1,128,2048]{2,1,0:T(8,128)(4,1)S(1)}, pred[1,128,2048]{2,1,0:T(8,128)(4,1)}, u32[]{:S(2)}) copy-start(pred[1,128,2048]{2,1,0:T(8,128)(4,1)} %get-tuple-element.70) | copy-start | bytes 786436
  235.7 5.0 copy-start.38
  235.7 5.0 copy-start.39
  235.7 5.0 copy-start.40
  235.7 5.0 copy-start.41
  235.7 5.0 copy-start.42
  235.8 5.0 copy-start.43
  235.8 5.0 copy-start.44
  235.8 5.0 copy-start.45
  339.2 15.5 %copy-start.54 = (f32[128]{0:T(128)S(1)}, f32[128]{0:T(128)}, u32[]{:S(2)}) copy-start(f32[128]{0:T(128)} %copy-done.53) | copy-start | bytes 1540
  339.4 22.9 %copy-start.56 = (f32[128]{0:T(128)S(1)}, f32[128]{0:T(128)}, u32[]{:S(2)}) copy-start(f32[128]{0:T(128)} %copy-done.55) | copy-start | bytes 1540
  385.5 3.8 copy-start.73
  385.5 3.9 copy-start.82
  412.4 26.0 %copy-start.9 = (f32[128,2048]{1,0:T(8,128)S(1)}, f32[128,2048]{1,0:T(8,128)}, u32[]{:S(2)}) copy-start(f32[128,2048]{1,0:T(8,128)} %get-tuple-element.315) | copy-start | bytes 3145732
  (43 other events, 111.2 us)

commit v2 on v1

--- a/solution.py
+++ b/solution.py
@@ -1,11 +1,15 @@
-import math
+from functools import partial
+
 import jax
 import jax.numpy as jnp
 from jax import lax
+from jax.experimental import pallas as pl
+from jax.experimental.pallas import tpu as pltpu
 from jax.sharding import PartitionSpec as P
 
 STEPS = 2
 BLOCK = 128
+INTERPRET = False
 HIGHEST = lax.Precision.HIGHEST
 
 
@@ -176,9 +180,539 @@
     return jnp.stack(u)[None]
 
 
+F32 = jnp.float32
+BF16 = jnp.bfloat16
+LHS_ROWS = 272
+CHUNK = 32
+VMEM_LIMIT = 56 * 1024 * 1024
+
+
+def tile_of(value):
+    return jnp.full((8, BLOCK), value, F32)
+
+
+def grid_power(base, exponent, bits):
+    real = jnp.ones(exponent.shape, F32)
+    imaginary = jnp.zeros(exponent.shape, F32)
+    for bit in range(bits):
+        on = (exponent // (1 << bit)) % 2 == 1
+        step = c_mul((real, imaginary), base)
+        real = jnp.where(on, step[0], real)
+        imaginary = jnp.where(on, step[1], imaginary)
+        base = c_mul(base, base)
+    return real, imaginary
+
+
+def spread_to(pair, shape):
+    return tuple(jnp.broadcast_to(part[0:1, 0:1], shape) for part in pair)
+
+
+def prepare_kernel(total, number_ref, length_ref, offset_ref, zone_ref, matrix_ref, column_ref, row_ref):
+    mine = lax.axis_index("sect")
+    number = tile_of(number_ref[mine])
+    tall = (BLOCK, BLOCK)
+    place = lax.broadcasted_iota(jnp.int32, tall, 0)
+    across = lax.broadcasted_iota(jnp.int32, tall, 1)
+    lane = lax.broadcasted_iota(jnp.int32, (8, BLOCK), 1)
+    lens = zone_ref[pl.ds(mine, 1), :]
+    for section in range(2):
+        length = tile_of(length_ref[section])
+        sigma = number * length * 0.25
+        size = 0.0625 + sigma * sigma
+        square = number * number / size
+        z = (-0.0625 * square, -0.25 * sigma * square)
+        sinh = c_sqrt(z)
+        cosh = c_sqrt((1.0 + z[0], z[1]))
+        root = (cosh[0] - sinh[0], cosh[1] - sinh[1])
+        base = c_mul(root, root)
+        gamma = c_mul((-2.0 * sigma * sigma / size, -0.5 * sigma / size), c_div(sinh, cosh))
+        alpha = ((0.0625 - sigma * sigma) / size, 0.5 * sigma / size)
+        turn = c_mul(alpha, alpha)
+        hop = base
+        for _ in range(7):
+            hop = c_mul(hop, hop)
+        whole = hop
+        for _ in range(total.bit_length() - 8):
+            whole = c_mul(whole, whole)
+        close = c_div((jnp.ones_like(whole[0]), jnp.zeros_like(whole[0])), (1.0 - whole[0], -whole[1]))
+        wide = spread_to(base, tall)
+        gain = spread_to(gamma, tall)
+        real, imaginary = c_mul(gain, grid_power(wide, jnp.abs(place - across), 7))
+        real = real + jnp.where(place == across, 1.0, 0.0)
+        matrix_ref[section, 0:128, 0:128] = real
+        matrix_ref[section, 0:128, 128:256] = -imaginary
+        matrix_ref[section, 128:256, 0:128] = imaginary
+        matrix_ref[section, 128:256, 128:256] = real
+        ahead = grid_power(base, lane, 7)
+        behind = grid_power(base, 127 - lane, 7)
+        left = c_mul(gamma, behind)
+        right = c_mul(gamma, ahead)
+        zero = jnp.zeros((1, BLOCK), F32)
+        rows = (left, right)
+        for index, weight in enumerate(rows):
+            matrix_ref[section, 256 + 2 * index : 257 + 2 * index, 0:128] = weight[0][0:1]
+            matrix_ref[section, 256 + 2 * index : 257 + 2 * index, 128:256] = -weight[1][0:1]
+            matrix_ref[section, 257 + 2 * index : 258 + 2 * index, 0:128] = weight[1][0:1]
+            matrix_ref[section, 257 + 2 * index : 258 + 2 * index, 128:256] = weight[0][0:1]
+        matrix_ref[section, 260:384, :] = jnp.zeros((124, 256), F32)
+        phase = number * length * jnp.broadcast_to(offset_ref[section : section + 1, :], (8, BLOCK))
+        screen = c_mul(turn, (jnp.cos(phase), jnp.sin(phase)))
+        reach_left = c_mul(base, ahead)
+        reach_right = c_mul(base, behind)
+        listed = [screen[0], screen[1], jnp.broadcast_to(jnp.cos(lens), (8, BLOCK)), jnp.broadcast_to(jnp.sin(lens), (8, BLOCK))]
+        listed += [reach_left[0], reach_left[1], reach_right[0], reach_right[1], hop[0], hop[1], close[0], close[1]]
+        both = c_mul(gamma, hop)
+        listed += [both[0], both[1]]
+        for index, value in enumerate(listed):
+            row_ref[section, 8 * index : 8 * index + 8, :] = value
+        down = grid_power(wide, place, 7)
+        up = grid_power(wide, 127 - place, 7)
+        high = c_mul(wide, down)
+        low = c_mul(wide, up)
+        from_left = c_mul(gain, up)
+        from_right = c_mul(gain, down)
+        tables = [high, low, from_left, from_right, c_mul(from_left, low), c_mul(from_right, high)]
+        for index, table in enumerate(tables):
+            column_ref[section, 2 * index] = table[0]
+            column_ref[section, 2 * index + 1] = table[1]
+
+
+def split(value):
+    high = value.astype(BF16)
+    return high, (value - high.astype(F32)).astype(BF16)
+
+
+def set_matrix(matrix_ref, section, factor_ref):
+    high, low = split(matrix_ref[section, 0:LHS_ROWS, :])
+    factor_ref[section, :, 0:256] = high
+    factor_ref[section, :, 256:512] = low
+    factor_ref[section, :, 512:768] = high
+
+
+def put_operand(operand_ref, top, real, imaginary):
+    size = real.shape[0]
+    high, low = split(real)
+    operand_ref[top : top + size, 0:128] = high
+    operand_ref[top : top + size, 256:384] = low
+    high, low = split(imaginary)
+    operand_ref[top : top + size, 128:256] = high
+    operand_ref[top : top + size, 384:512] = low
+
+
+def multiply(factor_ref, section, operand_ref):
+    high = operand_ref[:, 0:256]
+    right = jnp.concatenate([high, high, operand_ref[:, 256:512]], axis=1)
+    return lax.dot_general(factor_ref[section], right, (((1,), (1,)), ((), ())), preferred_element_type=F32)
+
+
+def pick(table_ref, section, index, labels):
+    table = jnp.broadcast_to(table_ref[section, 8 * index : 8 * index + 1, :], labels.shape)
+    return jnp.take_along_axis(table, labels, axis=1, mode="promise_in_bounds")
+
+
+def row_line(row_ref, section, index):
+    return row_ref[section, 8 * index : 8 * index + 1, :]
+
+
+def hop_of(row_ref, section):
+    return (row_line(row_ref, section, 8), row_line(row_ref, section, 9)), (row_line(row_ref, section, 10), row_line(row_ref, section, 11))
+
+
+def carries(get, put, count, hop, close):
+    for reverse in (False, True):
+        order = list(range(count))[:: -1 if reverse else 1]
+        total = get(order[0], reverse)
+        for index in order[1:]:
+            total = c_add(c_mul(hop, total), get(index, reverse))
+        carry = c_mul(close, total)
+        for index in order:
+            put(index, reverse, carry)
+            carry = c_add(c_mul(hop, carry), get(index, reverse))
+
+
+def scan_rows(edge_ref, carry_ref, row_ref, section, pairs):
+    hop, close = hop_of(row_ref, section)
+
+    def get(block, reverse):
+        first = 2 if reverse else 0
+        lanes = slice(128 * (block % 2), 128 * (block % 2) + 128)
+        return tuple(edge_ref[block // 2, first + part : first + part + 1, lanes] for part in range(2))
+
+    def put(block, reverse, value):
+        first = 2 if reverse else 0
+        for part in range(2):
+            carry_ref[block, first + part : first + part + 1, :] = value[part]
+
+    carries(get, put, 2 * pairs, hop, close)
+
+
+def add_reach(column_ref, section, rows, value, left, right):
+    high = (column_ref[section, 0, rows, :], column_ref[section, 1, rows, :])
+    low = (column_ref[section, 2, rows, :], column_ref[section, 3, rows, :])
+    return c_add(value, c_add(c_mul(high, left), c_mul(low, right)))
+
+
+def row_pass(section, operand_ref, factor_ref, grid_ref, edge_ref, pair):
+    out = multiply(factor_ref, section, operand_ref)
+    grid_ref[pair] = out[0:256]
+    edge_ref[pair] = out[256:264]
+
+
+def column_pass(section, operand_ref, factor_ref, column_ref, carry_ref, grid_ref, pair):
+    for half in range(2):
+        lanes = slice(128 * half, 128 * half + 128)
+        block = 2 * pair + half
+        line = [carry_ref[block, part : part + 1, :] for part in range(4)]
+        for top in range(0, BLOCK, CHUNK):
+            rows = slice(top, top + CHUNK)
+            value = (grid_ref[pair, rows, lanes], grid_ref[pair, top + 128 : top + 128 + CHUNK, lanes])
+            value = add_reach(column_ref, section, rows, value, (line[0], line[1]), (line[2], line[3]))
+            put_operand(operand_ref, 128 * half + top, *value)
+    return multiply(factor_ref, section, operand_ref)
+
+
+def pack_sums(section, value_ref, label_at, pair, row_ref, column_ref, ends, out_ref):
+    for half in range(2):
+        block = 2 * pair + half
+        lanes = slice(128 * half, 128 * half + 128)
+        sums = [jnp.zeros((8, BLOCK), F32) for _ in range(10)]
+        for top in range(0, BLOCK, 8):
+            rows = slice(top, top + 8)
+            labels = label_at(half, rows)
+            screen = (pick(row_ref, section, 0, labels), pick(row_ref, section, 1, labels))
+            value = c_mul(screen, (value_ref[rows, lanes], value_ref[top + 128 : top + 136, lanes]))
+            weights = [(column_ref[section, 2 * k, rows, :], column_ref[section, 2 * k + 1, rows, :]) for k in range(2, 6)]
+            terms = (c_mul(weights[0], value), c_mul(weights[1], value), screen, c_mul(weights[2], screen), c_mul(weights[3], screen))
+            for k, term in enumerate(terms):
+                sums[2 * k] = sums[2 * k] + term[0]
+                sums[2 * k + 1] = sums[2 * k + 1] + term[1]
+        lines = [jnp.sum(part, axis=0, keepdims=True) for part in sums]
+        both = c_mul((row_line(row_ref, section, 12), row_line(row_ref, section, 13)), (lines[4], lines[5]))
+        out_ref[block, 0:4, :] = ends[0:4, lanes]
+        for k, line in enumerate(lines[0:4] + list(both) + lines[6:10]):
+            out_ref[block, 4 + k : 5 + k, :] = line
+        out_ref[block, 14:16, :] = jnp.zeros((2, BLOCK), F32)
+
+
+def line_solve(section, back_ref, small_ref, line_ref, edge_ref, matrix_ref, row_ref, blocks):
+    small_ref[...] = jnp.zeros(small_ref.shape, F32)
+    for block in range(blocks):
+        for side in range(2):
+            for part in range(2):
+                row = 4 + 2 * side + part
+                small_ref[8 * block + side : 8 * block + side + 1, 128 * part : 128 * part + 128] = back_ref[block, row : row + 1, :]
+    high, low = split(small_ref[...])
+    factor_high, factor_low = split(matrix_ref[section])
+
+    def dot(a, b):
+        return lax.dot_general(a, b, (((1,), (1,)), ((), ())), preferred_element_type=F32)
+
+    out = dot(high, factor_high) + dot(low, factor_high) + dot(high, factor_low)
+    line_ref[...] = out
+    hop, close = hop_of(row_ref, section)
+    wide = (8, BLOCK)
+    hop = tuple(jnp.broadcast_to(part, wide) for part in hop)
+    close = tuple(jnp.broadcast_to(part, wide) for part in close)
+    reach_left = tuple(row_ref[section, 8 * k : 8 * k + 8, :] for k in (4, 5))
+    reach_right = tuple(row_ref[section, 8 * k : 8 * k + 8, :] for k in (6, 7))
+
+    def get(block, reverse):
+        first = 258 if reverse else 256
+        rows = slice(8 * block, 8 * block + 8)
+        return tuple(jnp.broadcast_to(line_ref[rows, first + part : first + part + 1], wide) for part in range(2))
+
+    def put(block, reverse, value):
+        rows = slice(8 * block, 8 * block + 8)
+        add = c_mul(reach_right if reverse else reach_left, value)
+        line_ref[rows, 0:128] = line_ref[rows, 0:128] + add[0]
+        line_ref[rows, 128:256] = line_ref[rows, 128:256] + add[1]
+
+    carries(get, put, blocks, hop, close)
+
+
+def line_at(line_ref, block):
+    parts = []
+    rows = pl.ds(pl.multiple_of(8 * block, 8), 8)
+    for side in range(2):
+        for part in range(2):
+            parts.append(line_ref[rows, 128 * part : 128 * part + 128][side : side + 1])
+    return (parts[0], parts[1]), (parts[2], parts[3])
+
+
+def lanes_of(pair, half):
+    return pl.ds(pl.multiple_of(256 * pair + 128 * half, 128), 128)
+
+
+def first_kernel(pairs, field_any, own_any, other_any, matrix_ref, column_ref, row_ref, out_ref, sums_ref,
+                 field_ref, label_ref, factor_ref, operand_ref, grid_ref, edge_ref, carry_ref, value_ref, sems):
+    mine = lax.axis_index("sect")
+    copy = pltpu.make_async_copy(field_any.at[mine], field_ref, sems.at[0])
+    copy.start()
+
+    @pl.when(mine == 0)
+    def _():
+        pltpu.make_async_copy(own_any.at[0], label_ref, sems.at[1]).start()
+
+    @pl.when(mine != 0)
+    def _():
+        pltpu.make_async_copy(other_any.at[0], label_ref, sems.at[1]).start()
+
+    set_matrix(matrix_ref, 0, factor_ref)
+    copy.wait()
+    pltpu.make_async_copy(own_any.at[0], label_ref, sems.at[1]).wait()
+
+    def enter(pair, _):
+        for half in range(2):
+            for top in range(0, BLOCK, CHUNK):
+                rows = slice(top, top + CHUNK)
+                lanes = lanes_of(pair, half)
+                labels = label_ref[rows, lanes]
+                screen = (pick(row_ref, 0, 0, labels), pick(row_ref, 0, 1, labels))
+                value = c_mul(screen, (field_ref[0, rows, lanes], field_ref[1, rows, lanes]))
+                put_operand(operand_ref, 128 * half + top, *value)
+        row_pass(0, operand_ref, factor_ref, grid_ref, edge_ref, pair)
+        return 0
+
+    lax.fori_loop(0, pairs, enter, 0)
+    scan_rows(edge_ref, carry_ref, row_ref, 0, pairs)
+
+    def leave(pair, _):
+        value = column_pass(0, operand_ref, factor_ref, column_ref, carry_ref, grid_ref, pair)
+        value_ref[...] = value[0:264]
+        wide = pl.ds(pl.multiple_of(256 * pair, 256), 256)
+        out_ref[0, :, wide] = value[0:128]
+        out_ref[1, :, wide] = value[128:256]
+        pack_sums(0, value_ref, lambda half, rows: label_ref[rows, lanes_of(pair, half)], pair, row_ref, column_ref,
+                  value_ref[256:264, :], sums_ref)
+        return 0
+
+    lax.fori_loop(0, pairs, leave, 0)
+
+
+def middle_kernel(peers, section, held_ref, row_ref, back_ref):
+    hop, close = hop_of(row_ref, section)
+
+    def line(peer, row):
+        return held_ref[peer, row : row + 1, :], held_ref[peer, row + 1 : row + 2, :]
+
+    def keep(first):
+        def put(peer, reverse, value):
+            row = first + (2 if reverse else 0)
+            back_ref[peer, row : row + 1, :] = value[0]
+            back_ref[peer, row + 1 : row + 2, :] = value[1]
+
+        return put
+
+    carries(lambda peer, reverse: line(peer, 2 if reverse else 0), keep(0), peers, hop, close)
+
+    def later(peer, reverse):
+        left = (back_ref[peer, 0:1, :], back_ref[peer, 1:2, :])
+        right = (back_ref[peer, 2:3, :], back_ref[peer, 3:4, :])
+        if reverse:
+            return c_add(line(peer, 6), c_add(c_mul(line(peer, 12), left), c_mul(line(peer, 8), right)))
+        return c_add(line(peer, 4), c_add(c_mul(line(peer, 8), left), c_mul(line(peer, 10), right)))
+
+    carries(later, keep(4), peers, hop, close)
+
+
+def take_in(section, pair, value_ref, label_ref, back_ref, column_ref, row_ref, operand_ref):
+    for half in range(2):
+        block = 2 * pair + half
+        lanes = lanes_of(pair, half)
+        line = [back_ref[block, part : part + 1, :] for part in range(4)]
+        for top in range(0, BLOCK, CHUNK):
+            rows = slice(top, top + CHUNK)
+            value = (value_ref[0, rows, lanes], value_ref[1, rows, lanes])
+            value = add_reach(column_ref, section, rows, value, (line[0], line[1]), (line[2], line[3]))
+            labels = label_ref[rows, lanes]
+            value = c_mul((pick(row_ref, section, 0, labels), pick(row_ref, section, 1, labels)), value)
+            put_operand(operand_ref, 128 * half + top, *value)
+
+
+def second_kernel(pairs, value_in, back_ref, own_any, other_any, zone_ref, matrix_ref, column_ref, row_ref, out_ref, sums_ref,
+                  label_ref, factor_ref, operand_ref, grid_ref, edge_ref, carry_ref, value_ref, small_ref, line_ref, sems):
+    mine = lax.axis_index("sect")
+
+    @pl.when(mine == 0)
+    def _():
+        pltpu.make_async_copy(own_any.at[0], label_ref.at[0], sems.at[0]).start()
+        pltpu.make_async_copy(other_any.at[0], label_ref.at[1], sems.at[1]).start()
+
+    @pl.when(mine != 0)
+    def _():
+        pltpu.make_async_copy(other_any.at[0], label_ref.at[0], sems.at[0]).start()
+        pltpu.make_async_copy(own_any.at[0], label_ref.at[1], sems.at[1]).start()
+
+    for section in range(2):
+        set_matrix(matrix_ref, section, factor_ref)
+    line_solve(0, back_ref, small_ref, line_ref, edge_ref, matrix_ref, row_ref, 2 * pairs)
+    pltpu.make_async_copy(own_any.at[0], label_ref.at[0], sems.at[0]).wait()
+    pltpu.make_async_copy(own_any.at[0], label_ref.at[1], sems.at[1]).wait()
+
+    def enter(pair, _):
+        take_in(0, pair, value_in, label_ref.at[0], back_ref, column_ref, row_ref, operand_ref)
+        row_pass(0, operand_ref, factor_ref, grid_ref, edge_ref, pair)
+        return 0
+
+    lax.fori_loop(0, pairs, enter, 0)
+    scan_rows(edge_ref, carry_ref, row_ref, 0, pairs)
+
+    def turn(pair, _):
+        value_ref[...] = column_pass(0, operand_ref, factor_ref, column_ref, carry_ref, grid_ref, pair)[0:264]
+        for half in range(2):
+            block = 2 * pair + half
+            inner = slice(128 * half, 128 * half + 128)
+            lanes = lanes_of(pair, half)
+            left, right = line_at(line_ref, block)
+            for top in range(0, BLOCK, CHUNK):
+                rows = slice(top, top + CHUNK)
+                value = (value_ref[rows, inner], value_ref[top + 128 : top + 128 + CHUNK, inner])
+                value = add_reach(column_ref, 0, rows, value, left, right)
+                labels = label_ref[1, rows, lanes]
+                value = c_mul((pick(row_ref, 1, 0, labels), pick(row_ref, 1, 1, labels)), value)
+                zones = zone_ref[rows, lanes]
+                value = c_mul((pick(row_ref, 1, 2, zones), pick(row_ref, 1, 3, zones)), value)
+                put_operand(operand_ref, 128 * half + top, *value)
+        row_pass(1, operand_ref, factor_ref, grid_ref, edge_ref, pair)
+        return 0
+
+    lax.fori_loop(0, pairs, turn, 0)
+    scan_rows(edge_ref, carry_ref, row_ref, 1, pairs)
+
+    def leave(pair, _):
+        value = column_pass(1, operand_ref, factor_ref, column_ref, carry_ref, grid_ref, pair)
+        value_ref[...] = value[0:264]
+        wide = pl.ds(pl.multiple_of(256 * pair, 256), 256)
+        out_ref[0, :, wide] = value[0:128]
+        out_ref[1, :, wide] = value[128:256]
+        pack_sums(1, value_ref, lambda half, rows: label_ref[1, rows, lanes_of(pair, half)], pair, row_ref, column_ref,
+                  value_ref[256:264, :], sums_ref)
+        return 0
+
+    lax.fori_loop(0, pairs, leave, 0)
+
+
+def third_kernel(pairs, value_in, back_ref, own_any, other_any, matrix_ref, column_ref, row_ref, out_ref,
+                 label_ref, factor_ref, operand_ref, grid_ref, edge_ref, carry_ref, value_ref, small_ref, line_ref, sems):
+    mine = lax.axis_index("sect")
+
+    @pl.when(mine == 0)
+    def _():
+        pltpu.make_async_copy(other_any.at[0], label_ref, sems.at[0]).start()
+
+    @pl.when(mine != 0)
+    def _():
+        pltpu.make_async_copy(own_any.at[0], label_ref, sems.at[0]).start()
+
+    set_matrix(matrix_ref, 1, factor_ref)
+    line_solve(1, back_ref, small_ref, line_ref, edge_ref, matrix_ref, row_ref, 2 * pairs)
+    pltpu.make_async_copy(own_any.at[0], label_ref, sems.at[0]).wait()
+
+    def enter(pair, _):
+        take_in(1, pair, value_in, label_ref, back_ref, column_ref, row_ref, operand_ref)
+        row_pass(1, operand_ref, factor_ref, grid_ref, edge_ref, pair)
+        return 0
+
+    lax.fori_loop(0, pairs, enter, 0)
+    scan_rows(edge_ref, carry_ref, row_ref, 1, pairs)
+
+    def leave(pair, _):
+        value_ref[...] = column_pass(1, operand_ref, factor_ref, column_ref, carry_ref, grid_ref, pair)[0:264]
+        for half in range(2):
+            block = 2 * pair + half
+            inner = slice(128 * half, 128 * half + 128)
+            lanes = lanes_of(pair, half)
+            left, right = line_at(line_ref, block)
+            for top in range(0, BLOCK, CHUNK):
+                rows = slice(top, top + CHUNK)
+                value = (value_ref[rows, inner], value_ref[top + 128 : top + 128 + CHUNK, inner])
+                value = add_reach(column_ref, 1, rows, value, left, right)
+                out_ref[0, 0, rows, lanes] = value[0]
+                out_ref[0, 1, rows, lanes] = value[1]
+        return 0
+
+    lax.fori_loop(0, pairs, leave, 0)
+
+
+ANY = pl.BlockSpec(memory_space=pl.ANY)
+VMEM = pl.BlockSpec(memory_space=pltpu.VMEM)
+SMEM = pl.BlockSpec(memory_space=pltpu.SMEM)
+
+
+def call(body, in_specs, out_shape, scratch=()):
+    out_specs = jax.tree.map(lambda _: VMEM, out_shape)
+    return pl.pallas_call(
+        body,
+        in_specs=in_specs,
+        out_specs=out_specs,
+        out_shape=out_shape,
+        scratch_shapes=list(scratch),
+        compiler_params=pltpu.CompilerParams(vmem_limit_bytes=VMEM_LIMIT),
+        interpret=INTERPRET,
+    )
+
+
+def fast_shards(fields, region_ids, index_offsets, step_lengths, wave_numbers, zone_ids, zone_phases):
+    peers = lax.axis_size("slab")
+    width = fields.shape[-1]
+    pairs = width // 256
+    other = lax.ppermute(region_ids, "sect", [(0, 1), (1, 0)])
+
+    def shape(*sizes):
+        return jax.ShapeDtypeStruct(sizes, F32)
+
+    def padded(table):
+        return jnp.pad(table, ((0, 0), (0, BLOCK - table.shape[1])))
+
+    matrix, column, row = call(
+        partial(prepare_kernel, width),
+        [SMEM, SMEM, VMEM, VMEM],
+        (shape(2, 384, 256), shape(2, 12, BLOCK, BLOCK), shape(2, 8 * 14, BLOCK)),
+    )(wave_numbers, step_lengths, padded(index_offsets), padded(zone_phases))
+    solve = [
+        pltpu.VMEM((2, LHS_ROWS, 768), BF16),
+        pltpu.VMEM((256, 512), BF16),
+        pltpu.VMEM((pairs, 256, 256), F32),
+        pltpu.VMEM((pairs, 8, 256), F32),
+        pltpu.VMEM((2 * pairs, 8, BLOCK), F32),
+        pltpu.VMEM((264, 256), F32),
+    ]
+    small = [pltpu.VMEM((16 * pairs, 256), F32), pltpu.VMEM((16 * pairs, 384), F32)]
+    labels = pltpu.VMEM((BLOCK, width), jnp.int32)
+    sems = pltpu.SemaphoreType.DMA((2,))
+    grids = (shape(2, BLOCK, width), shape(peers, 16, BLOCK))
+
+    def exchange(sums, section):
+        held = lax.all_to_all(sums, "slab", 0, 0, tiled=True)
+        back = call(partial(middle_kernel, peers, section), [VMEM, VMEM], shape(peers, 8, BLOCK))(held, row)
+        return lax.all_to_all(back, "slab", 0, 0, tiled=True)
+
+    value, sums = call(
+        partial(first_kernel, pairs), [ANY, ANY, ANY, VMEM, VMEM, VMEM], grids,
+        [pltpu.VMEM((2, BLOCK, width), F32), labels] + solve + [sems],
+    )(fields, region_ids, other, matrix, column, row)
+    back = exchange(sums, 0)
+    value, sums = call(
+        partial(second_kernel, pairs), [VMEM, VMEM, ANY, ANY, VMEM, VMEM, VMEM, VMEM], grids,
+        [pltpu.VMEM((2, BLOCK, width), jnp.int32)] + solve + small + [sems],
+    )(value, back, region_ids, other, zone_ids, matrix, column, row)
+    back = exchange(sums, 1)
+    return call(
+        partial(third_kernel, pairs), [VMEM, VMEM, ANY, ANY, VMEM, VMEM, VMEM], shape(1, 2, BLOCK, width),
+        [labels] + solve + small + [sems],
+    )(value, back, region_ids, other, matrix, column, row)
+
+
+def choose(fields, *others):
+    rows, width = fields.shape[-2:]
+    if rows == BLOCK and width == BLOCK * lax.axis_size("slab") and lax.axis_size("sect") == 2:
+        return fast_shards(fields, *others)
+    return shards(fields, *others)
+
+
 def solution(mesh):
     return jax.shard_map(
-        shards,
+        choose,
         mesh=mesh,
         in_specs=(
             P(None, None, "slab", None),

time: 532 us -> 108 us (0.20); the launches traced: 525 us -> 108 us
  matrix products: 326 us -> 0 us
  other arithmetic: 125 us -> 0 us
  Pallas kernels: 0 us -> 52.4 us
  blocking collectives: 22.1 us -> 51.4 us
  local copies, waits for them, and re-layouts: 22.2 us -> 3.49 us
  starting transfers between devices: 11.8 us -> 0.45 us
  between operations: 8.57 us -> 0.02 us
  waiting for transfers between devices: 8.34 us -> 0.01 us
    dot_general x264 -> x0, matrix products: 326 us -> none  [one(): return jnp.einsum(spec, x, y, precision=HIGHEST)]
    add x27 -> x0, other arithmetic: 106 us -> none  [the longest x9 82.3 us: c_mul(): return (a[0] * b[0] - a[1] * b[1], a[0] * b[1] + a[1] * b[0])]
    pallas_call x0 -> x6, Pallas kernels: none -> 52.4 us  [the longest x1 20.6 us: fast_shards(): call(partial(second_kernel, pairs), [VMEM, VMEM, ANY, ANY, VMEM, VMEM, VM...]
    all_to_all x2 -> x4, blocking collectives: 22.1 us -> 51.4 us  [the longest x2 28.1 us: exchange(): held = lax.all_to_all(sums, 'slab', 0, 0, tiled=True)]
    eq x3 -> x0, other arithmetic: 13.9 us -> none  [pick_values(): picked = picked + jnp.where(labels == entry, table[entry], 0.0)]
    all_to_all x2 -> x0, starting transfers between devices: 11.3 us -> none  [the longest x1 7.86 us: exchange(): held = lax.all_to_all(sent, 'slab', 0, 0, tiled=True)]
    all_to_all x2 -> x0, waiting for transfers between devices: 8.34 us -> none  [the longest x1 5.64 us: exchange(): held = lax.all_to_all(sent, 'slab', 0, 0, tiled=True)]
    slice x13 -> x0, local copies, waits for them, and re-layouts: 7.37 us -> none  [the longest x8 5.75 us: pick_values(): picked = picked + jnp.where(labels == entry, table[entry], 0.0)]
  transfers between devices with their start and end apart: 3 -> 1, of which waited for: 2 -> 0; matrix products, arithmetic and copies ran while one was open for 6% -> 2% of each run, Pallas kernels for 0% -> 3%
where the time goes in v2:
time: 108 us
  Pallas kernels  52.4 us (49%)
  blocking collectives  51.4 us (48%)
  local copies, waits for them, and re-layouts  3.49 us (3%)
    all_to_all x2, blocking collectives, exchange(): held = lax.all_to_all(sums, 'slab', 0, 0, tiled=True)  28.1 us
    all_to_all x2, blocking collectives, exchange(): return lax.all_to_all(back, 'slab', 0, 0, tiled=True)  23.4 us
    pallas_call x1, Pallas kernels, fast_shards(): call(partial(second_kernel, pairs), [VMEM, VMEM, ANY, ANY, VMEM, VMEM, VM...  20.6 us
    pallas_call x1, Pallas kernels, fast_shards(): call(partial(first_kernel, pairs), [ANY, ANY, ANY, VMEM, VMEM, VMEM], gri...  12.7 us
    pallas_call x1, Pallas kernels, fast_shards(): call(partial(third_kernel, pairs), [VMEM, VMEM, ANY, ANY, VMEM, VMEM, VME...  12.1 us
    pallas_call x2, Pallas kernels, exchange(): call(partial(middle_kernel, peers, section), [VMEM, VMEM], shape(peers, 8...  3.82 us
    pallas_call x1, Pallas kernels, fast_shards(): call(partial(prepare_kernel, width), [SMEM, SMEM, VMEM, VMEM], (shape(2,...  3.1 us
    pad x2, local copies, waits for them, and re-layouts, padded(): return jnp.pad(table, ((0, 0), (0, BLOCK - table.shape[1])))  2.52 us
  transfers between devices with their start and end apart: 1, of which 0 were waited for; matrix products, arithmetic and copies ran while one was open for 2% of the time, Pallas kernels for 3%

profile of v2, /device:TPU:0, one launch (start us, length us, event | category | flops | bytes accessed | tf_op | source)
XLA Modules:
  0.0 107.8 jit_solution(6711823873511582030)
XLA Ops:
  0.0 0.5 collective-permute-start
  0.5 1.2 %pad.8.offset_ref = f32[2,128]{1,0:T(2,128)} pad(f32[2,16]{1,0:T(2,128)} %param.9, f32[]{:T(128)} %constant.2.clone.1), padding=0_0x0_112 | pad | bytes 1156 | tf_op jit(solution)/shard_map/jit(_pad)/pad | solution.py:665
  1.7 1.3 %pad.9.zone_ref = f32[2,128]{1,0:T(2,128)} pad(f32[2,32]{1,0:T(2,128)} %param.13, f32[]{:T(128)} %constant.2.clone.1), padding=0_0x0_96 | pad | bytes 1284 | tf_op jit(solution)/shard_map/jit(_pad)/pad | solution.py:665
  3.0 3.1 %shard_map.73 = (f32[2,384,256]{2,1,0:T(8,128)}, f32[2,12,128,128]{3,2,1,0:T(8,128)}, f32[2,112,128]{2,1,0:T(8,128)}) custom-call(f32[2]{0:T(128)} %number_ref.1, f32[2]{0:T(128)} %length_ref.1, f32[2,128]{1,0:T(2,128)} %pad.8.offset_ref, f32[2,128]{1,0:T(2,128)} %pad.9.zone_ref), custom_call_target="tpu_custom_call" | custom-call | tf_op jit(solution)/shard_map/pallas_call | solution.py:667
  6.1 0.0 collective-permute-done.other_any
  6.1 0.0 copy-start
  6.1 1.0 copy-done
  7.1 12.7 %shard_map.74 = (f32[2,128,2048]{2,1,0:T(8,128)}, f32[16,16,128]{2,1,0:T(8,128)}) custom-call(f32[2,2,128,2048]{3,2,1,0:T(8,128)} %field_any.1, s32[1,128,2048]{2,1,0:T(8,128)} %own_any.5, s32[1,128,2048]{2,1,0:T(8,128)} %copy-done, f32[2,384,256]{2,1,0:T(8,128)} %get-tuple-element.12.matrix_ref, f32[2,12,128,128]{3,2,1,0:T(8,128)} %get-tuple-element.13.column_ref, ...), custom_call_target="tpu_custom_call" | custom-call | tf_op jit(solution)/shard_map/pallas_call | solution.py:690
  19.8 16.1 %all_to_all.20.held_ref = f32[16,16,128]{2,1,0:T(8,128)} all-to-all(f32[16,16,128]{2,1,0:T(8,128)} %get-tuple-element.16), channel_id=1, replica_groups=mesh['slab'=16,'sect'=2] {'slab'}, dimensions={0} | all-to-all | bytes 262144 | tf_op jit(solution)/shard_map/all_to_all | solution.py:686
  35.9 1.9 %shard_map.75 = f32[16,8,128]{2,1,0:T(8,128)} custom-call(f32[16,16,128]{2,1,0:T(8,128)} %all_to_all.20.held_ref, f32[2,112,128]{2,1,0:T(8,128)} %get-tuple-element.14.row_ref), custom_call_target="tpu_custom_call" | custom-call | tf_op jit(solution)/shard_map/pallas_call | solution.py:687
  37.8 11.7 %all_to_all.21.back_ref = f32[16,8,128]{2,1,0:T(8,128)} all-to-all(f32[16,8,128]{2,1,0:T(8,128)} %shard_map.75), channel_id=1, replica_groups=mesh['slab'=16,'sect'=2] {'slab'}, dimensions={0} | all-to-all | bytes 131072 | tf_op jit(solution)/shard_map/all_to_all | solution.py:688
  49.5 20.6 %shard_map.76 = (f32[2,128,2048]{2,1,0:T(8,128)}, f32[16,16,128]{2,1,0:T(8,128)}) custom-call(f32[2,128,2048]{2,1,0:T(8,128)} %get-tuple-element.15.value_in, f32[16,8,128]{2,1,0:T(8,128)} %all_to_all.21.back_ref, s32[1,128,2048]{2,1,0:T(8,128)} %own_any.5, s32[1,128,2048]{2,1,0:T(8,128)} %copy-done, s32[128,2048]{1,0:T(8,128)} %zone_ref.1, ...), custom_call_target="tpu_custom_call" | custom-call | tf_op jit(solution)/shard_map/pallas_call | solution.py:695
  70.1 12.0 %all_to_all.22.held_ref = f32[16,16,128]{2,1,0:T(8,128)} all-to-all(f32[16,16,128]{2,1,0:T(8,128)} %get-tuple-element.18), channel_id=1, replica_groups=mesh['slab'=16,'sect'=2] {'slab'}, dimensions={0} | all-to-all | bytes 262144 | tf_op jit(solution)/shard_map/all_to_all | solution.py:686
  82.1 1.9 %shard_map.77 = f32[16,8,128]{2,1,0:T(8,128)} custom-call(f32[16,16,128]{2,1,0:T(8,128)} %all_to_all.22.held_ref, f32[2,112,128]{2,1,0:T(8,128)} %get-tuple-element.14.row_ref), custom_call_target="tpu_custom_call" | custom-call | tf_op jit(solution)/shard_map/pallas_call | solution.py:687
  84.0 11.7 %all_to_all.23.back_ref = f32[16,8,128]{2,1,0:T(8,128)} all-to-all(f32[16,8,128]{2,1,0:T(8,128)} %shard_map.77), channel_id=1, replica_groups=mesh['slab'=16,'sect'=2] {'slab'}, dimensions={0} | all-to-all | bytes 131072 | tf_op jit(solution)/shard_map/all_to_all | solution.py:688
  95.7 12.1 %shard_map.78 = f32[1,2,128,2048]{3,2,1,0:T(8,128)} custom-call(f32[2,128,2048]{2,1,0:T(8,128)} %get-tuple-element.17.value_in, f32[16,8,128]{2,1,0:T(8,128)} %all_to_all.23.back_ref, s32[1,128,2048]{2,1,0:T(8,128)} %own_any.5, s32[1,128,2048]{2,1,0:T(8,128)} %copy-done, f32[2,384,256]{2,1,0:T(8,128)} %get-tuple-element.12.matrix_ref, ...), custom_call_target="tpu_custom_call" | custom-call | tf_op jit(solution)/shard_map/pallas_call | solution.py:700
Async XLA Ops:
  0.0 6.1 %collective-permute-start = (s32[1,128,2048]{2,1,0:T(8,128)}, s32[1,128,2048]{2,1,0:T(8,128)S(1)}, u32[]{:S(2)}, u32[]{:S(2)}) collective-permute-start(s32[1,128,2048]{2,1,0:T(8,128)} %own_any.5), channel_id=1, source_target_pairs={{0,1},{1,0},{2,3},{3,2},{4,5},{5,4},{6,7},{7,6},{8,9},{9,8},{10,11... | collective-permute-start | bytes 3145736 | tf_op jit(solution)/shard_map/ppermute | solution.py:659
  6.1 1.0 copy-start

commit v3 on v2

v3 whole, which is shorter than its diff:
```python
from functools import partial

import jax
import jax.numpy as jnp
from jax import lax
from jax.experimental import pallas as pl
from jax.experimental.pallas import tpu as pltpu
from jax.sharding import PartitionSpec as P

STEPS = 2
BLOCK = 128
INTERPRET = False
HIGHEST = lax.Precision.HIGHEST


def c_mul(a, b):
    return a[0] * b[0] - a[1] * b[1], a[0] * b[1] + a[1] * b[0]


def c_add(a, b):
    return a[0] + b[0], a[1] + b[1]


def c_div(a, b):
    size = b[0] * b[0] + b[1] * b[1]
    return (a[0] * b[0] + a[1] * b[1]) / size, (a[1] * b[0] - a[0] * b[1]) / size


def c_sqrt(a):
    size = jnp.sqrt(a[0] * a[0] + a[1] * a[1])
    real = jnp.sqrt(0.5 * (size + a[0]))
    return real, 0.5 * a[1] / real


def c_power(theta, count):
    size = jnp.exp(-theta[0] * count)
    angle = theta[1] * count
    return size * jnp.cos(angle), -size * jnp.sin(angle)


def scalars(number, length):
    sigma = number * length * 0.25
    size = 0.0625 + sigma * sigma
    square = number * number / size
    z = (-0.0625 * square, -0.25 * sigma * square)
    sinh = c_sqrt(z)
    cosh = c_sqrt((1.0 + z[0], z[1]))
    small = c_add(sinh, c_div(z, (1.0 + cosh[0], cosh[1])))
    theta = (
        jnp.log1p(2.0 * small[0] + small[0] * small[0] + small[1] * small[1]),
        2.0 * jnp.arctan2(small[1], 1.0 + small[0]),
    )
    front = (-2.0 * sigma * sigma / size, -0.5 * sigma / size)
    gamma = c_mul(front, c_div(sinh, cosh))
    alpha = ((0.0625 - sigma * sigma) / size, 0.5 * sigma / size)
    return theta, gamma, c_mul(alpha, alpha)


def closure(theta, total):
    power = c_power(theta, float(total))
    return c_div((jnp.ones_like(power[0]), jnp.zeros_like(power[0])), (1.0 - power[0], -power[1]))


def toeplitz(theta, gamma, count):
    index = jnp.arange(count, dtype=jnp.int32)
    apart = jnp.abs(index[:, None] - index[None, :])
    real, imaginary = c_mul(gamma, c_power(theta, apart.astype(jnp.float32)))
    return jnp.where(apart == 0, 1.0, 0.0) + real, imaginary


def circulant(theta, size, blocks):
    index = jnp.arange(blocks, dtype=jnp.int32)
    apart = jnp.mod(index[:, None] - index[None, :] - 1, blocks).astype(jnp.float32)
    return c_mul(closure(theta, size * blocks), c_power(theta, apart * size))


def c_ein(spec, a, b):
    def one(x, y):
        return jnp.einsum(spec, x, y, precision=HIGHEST)

    return one(a[0], b[0]) - one(a[1], b[1]), one(a[0], b[1]) + one(a[1], b[0])


def spans(theta, gamma, count):
    index = jnp.arange(count, dtype=jnp.int32).astype(jnp.float32)
    weight_left = c_mul(gamma, c_power(theta, count - 1 - index))
    weight_right = c_mul(gamma, c_power(theta, index))
    reach_left = c_power(theta, index + 1)
    reach_right = c_power(theta, count - index)
    return weight_left, weight_right, reach_left, reach_right


def row_solve(x, theta, gamma):
    shape = x[0].shape
    blocks = shape[-1] // BLOCK
    x = tuple(part.reshape(shape[:-1] + (blocks, BLOCK)) for part in x)
    weight_left, weight_right, reach_left, reach_right = spans(theta, gamma, BLOCK)
    ring = circulant(theta, BLOCK, blocks)
    y = c_ein("...bi,ij->...bj", x, toeplitz(theta, gamma, BLOCK))
    left = c_ein("...b,cb->...c", c_ein("...bi,i->...b", x, weight_left), ring)
    right = c_ein("...b,bc->...c", c_ein("...bi,i->...b", x, weight_right), ring)
    y = c_add(y, c_ein("...b,i->...bi", left, reach_left))
    y = c_add(y, c_ein("...b,i->...bi", right, reach_right))
    return tuple(part.reshape(shape) for part in y)


def pick_values(labels, table):
    picked = jnp.zeros(labels.shape, jnp.float32)
    for entry in range(table.shape[-1]):
        picked = picked + jnp.where(labels == entry, table[entry], 0.0)
    return picked


def column_local(x, theta, gamma, rows):
    weight_left, weight_right, _, _ = spans(theta, gamma, rows)
    y = c_ein("ij,jm->im", toeplitz(theta, gamma, rows), x)
    return y, c_ein("i,im->m", weight_left, x), c_ein("i,im->m", weight_right, x)


def reach(y, left, right, theta, gamma, rows):
    _, _, reach_left, reach_right = spans(theta, gamma, rows)
    y = c_add(y, c_ein("i,m->im", reach_left, left))
    return c_add(y, c_ein("i,m->im", reach_right, right))


def payload(y, left, right, screen, theta, gamma, rows):
    weight_left, weight_right, reach_left, reach_right = spans(theta, gamma, rows)
    z = c_mul(screen, y)
    parts = [left, right, c_ein("i,im->m", weight_left, z), c_ein("i,im->m", weight_right, z)]
    for weight, other in ((weight_left, reach_left), (weight_left, reach_right), (weight_right, reach_left)):
        parts.append(c_ein("i,im->m", c_mul(weight, other), screen))
    return jnp.stack([half for part in parts for half in part])


def exchange(packed, theta, rows):
    peers = lax.axis_size("slab")
    width = packed.shape[-1] // peers
    sent = jnp.swapaxes(packed.reshape(packed.shape[0], peers, width), 0, 1)
    held = lax.all_to_all(sent, "slab", 0, 0, tiled=True)
    one = [(held[:, 2 * i], held[:, 2 * i + 1]) for i in range(7)]
    ring = circulant(theta, rows, peers)
    left = c_ein("cb,bm->cm", ring, one[0])
    right = c_ein("bc,bm->cm", ring, one[1])
    next_left = c_add(one[2], c_add(c_mul(one[4], left), c_mul(one[5], right)))
    next_right = c_add(one[3], c_add(c_mul(one[6], left), c_mul(one[4], right)))
    next_left = c_ein("cb,bm->cm", ring, next_left)
    next_right = c_ein("bc,bm->cm", ring, next_right)
    back = jnp.stack([half for part in (left, right, next_left, next_right) for half in part], axis=1)
    back = lax.all_to_all(back, "slab", 0, 0, tiled=True)
    back = jnp.swapaxes(back, 0, 1).reshape(8, peers * width)
    return [(back[2 * i], back[2 * i + 1]) for i in range(4)]


def shards(fields, region_ids, index_offsets, step_lengths, wave_numbers, zone_ids, zone_phases):
    mine = lax.axis_index("sect")
    other = lax.ppermute(region_ids, "sect", [(0, 1), (1, 0)])
    labels = [jnp.where(mine == s, region_ids[0], other[0]) for s in range(2)]
    field = lax.dynamic_index_in_dim(fields, mine, 0, False)
    number = lax.dynamic_index_in_dim(wave_numbers, mine, 0, False)
    phases = lax.dynamic_index_in_dim(zone_phases, mine, 0, False)
    rows = field.shape[1]
    u = (field[0], field[1])
    lens = (pick_values(zone_ids, jnp.cos(phases)), pick_values(zone_ids, jnp.sin(phases)))
    for section in range(2):
        theta, gamma, turn = scalars(number, step_lengths[section])
        phase = number * step_lengths[section] * index_offsets[section]
        table = c_mul(turn, (jnp.cos(phase), jnp.sin(phase)))
        screen = tuple(pick_values(labels[section], half) for half in table)
        u = c_mul(u, screen)
        if section == 1:
            u = c_mul(u, lens)
        u, left, right = column_local(row_solve(u, theta, gamma), theta, gamma, rows)
        sent = payload(u, left, right, screen, theta, gamma, rows)
        back = exchange(sent, theta, rows)
        u = reach(u, back[0], back[1], theta, gamma, rows)
        u, _, _ = column_local(row_solve(c_mul(u, screen), theta, gamma), theta, gamma, rows)
        left = row_solve(back[2], theta, gamma)
        right = row_solve(back[3], theta, gamma)
        u = reach(u, left, right, theta, gamma, rows)
    return jnp.stack(u)[None]


F32 = jnp.float32
BF16 = jnp.bfloat16
LHS_ROWS = 272
LOADS = 1
SLOTS = 2

CHUNK = 32
VMEM_LIMIT = 22 * 1024 * 1024


def tile_of(value):
    return jnp.full((8, BLOCK), value, F32)


def grid_power(base, exponent, bits):
    real = jnp.ones(exponent.shape, F32)
    imaginary = jnp.zeros(exponent.shape, F32)
    for bit in range(bits):
        on = (exponent // (1 << bit)) % 2 == 1
        step = c_mul((real, imaginary), base)
        real = jnp.where(on, step[0], real)
        imaginary = jnp.where(on, step[1], imaginary)
        base = c_mul(base, base)
    return real, imaginary


def spread_to(pair, shape):
    return tuple(jnp.broadcast_to(part[0:1, 0:1], shape) for part in pair)


def prepare_kernel(total, number_ref, length_ref, offset_ref, zone_ref, factor_ref, weight_ref, row_ref, pad_ref):
    mine = lax.axis_index("sect")
    number = tile_of(number_ref[mine])
    tall = (BLOCK, BLOCK)
    place = lax.broadcasted_iota(jnp.int32, tall, 0)
    across = lax.broadcasted_iota(jnp.int32, tall, 1)
    lane = lax.broadcasted_iota(jnp.int32, (8, BLOCK), 1)
    pad_ref[...] = jnp.zeros((8, BLOCK), F32)
    pad_ref[0:2, 0 : offset_ref.shape[1]] = offset_ref[...]
    pad_ref[2:3, 0 : zone_ref.shape[1]] = zone_ref[pl.ds(mine, 1), :]
    lens = jnp.broadcast_to(pad_ref[2:3, :], (8, BLOCK))
    lens = (jnp.cos(lens), jnp.sin(lens))

    def keep(section, top, bottom, real, imaginary):
        for first, value in ((0, real), (BLOCK, imaginary)):
            high, low = split(value)
            factor_ref[section, top:bottom, first : first + BLOCK] = high
            factor_ref[section, top:bottom, 256 + first : 256 + first + BLOCK] = low
            factor_ref[section, top:bottom, 512 + first : 512 + first + BLOCK] = high

    for section in range(2):
        length = tile_of(length_ref[section])
        sigma = number * length * 0.25
        size = 0.0625 + sigma * sigma
        square = number * number / size
        z = (-0.0625 * square, -0.25 * sigma * square)
        sinh = c_sqrt(z)
        cosh = c_sqrt((1.0 + z[0], z[1]))
        root = (cosh[0] - sinh[0], cosh[1] - sinh[1])
        base = c_mul(root, root)
        gamma = c_mul((-2.0 * sigma * sigma / size, -0.5 * sigma / size), c_div(sinh, cosh))
        alpha = ((0.0625 - sigma * sigma) / size, 0.5 * sigma / size)
        turn = c_mul(alpha, alpha)
        hop = base
        for _ in range(7):
            hop = c_mul(hop, hop)
        whole = hop
        for _ in range(total.bit_length() - 8):
            whole = c_mul(whole, whole)
        close = c_div((jnp.ones_like(whole[0]), jnp.zeros_like(whole[0])), (1.0 - whole[0], -whole[1]))
        wide = spread_to(base, tall)
        gain = spread_to(gamma, tall)
        real, imaginary = c_mul(gain, grid_power(wide, jnp.abs(place - across), 7))
        real = real + jnp.where(place == across, 1.0, 0.0)
        keep(section, 0, 128, real, -imaginary)
        keep(section, 128, 256, imaginary, real)
        ahead = grid_power(base, lane, 7)
        behind = grid_power(base, 127 - lane, 7)
        left = c_mul(gamma, behind)
        right = c_mul(gamma, ahead)
        row = lax.broadcasted_iota(jnp.int32, (16, BLOCK), 0)

        def four(values):
            out = jnp.zeros((16, BLOCK), F32)
            for index, value in enumerate(values):
                out = jnp.where(row == index, jnp.broadcast_to(value[0:1], (16, BLOCK)), out)
            return out

        keep(section, 256, 272, four((left[0], left[1], right[0], right[1])), four((-left[1], left[0], -right[1], right[0])))
        factor_ref[section, 272:384, :] = jnp.zeros((112, 768), BF16)
        phase = number * length * jnp.broadcast_to(pad_ref[section : section + 1, :], (8, BLOCK))
        screen = c_mul(turn, (jnp.cos(phase), jnp.sin(phase)))
        reach_left = c_mul(base, ahead)
        reach_right = c_mul(base, behind)
        both = c_mul(gamma, hop)
        listed = [*screen, *lens, *reach_left, *reach_right, *hop, *close, *both]
        for index, value in enumerate(listed):
            row_ref[section, 8 * index : 8 * index + 8, :] = value
        down = grid_power(wide, place, 7)
        up = grid_power(wide, 127 - place, 7)
        high = c_mul(wide, down)
        low = c_mul(wide, up)
        from_left = c_mul(gain, up)
        from_right = c_mul(gain, down)
        tables = [high, low, from_left, from_right, c_mul(from_left, low), c_mul(from_right, high)]
        for index, table in enumerate(tables):
            weight_ref[section, 2 * index] = table[0]
            weight_ref[section, 2 * index + 1] = table[1]


def split(value):
    high = value.astype(BF16)
    return high, (value - high.astype(F32)).astype(BF16)


def put_operand(operand_ref, top, real, imaginary):
    size = real.shape[0]
    high, low = split(real)
    operand_ref[top : top + size, 0:128] = high
    operand_ref[top : top + size, 256:384] = low
    high, low = split(imaginary)
    operand_ref[top : top + size, 128:256] = high
    operand_ref[top : top + size, 384:512] = low


def multiply(factor_ref, section, operand_ref):
    high = operand_ref[:, 0:256]
    right = jnp.concatenate([high, high, operand_ref[:, 256:512]], axis=1)
    return lax.dot_general(factor_ref[section, 0:LHS_ROWS, :], right, (((1,), (1,)), ((), ())), preferred_element_type=F32)


def add_reach(weight_ref, section, rows, value, line):
    high = (weight_ref[section, 0, rows, :], weight_ref[section, 1, rows, :])
    low = (weight_ref[section, 2, rows, :], weight_ref[section, 3, rows, :])
    return c_add(value, c_add(c_mul(high, (line[0], line[1])), c_mul(low, (line[2], line[3]))))


def line_of(carry_ref, block):
    return [carry_ref[block, part : part + 1, :] for part in range(4)]


def pick(table_ref, section, index, labels):
    table = jnp.broadcast_to(table_ref[section, 8 * index : 8 * index + 1, :], labels.shape)
    return jnp.take_along_axis(table, labels, axis=1, mode="promise_in_bounds")


def screen_at(row_ref, section, labels):
    return pick(row_ref, section, 0, labels), pick(row_ref, section, 1, labels)


def row_line(row_ref, section, index):
    return row_ref[section, 8 * index : 8 * index + 1, :]


def hop_of(row_ref, section):
    return (row_line(row_ref, section, 8), row_line(row_ref, section, 9)), (row_line(row_ref, section, 10), row_line(row_ref, section, 11))


def carries(get, put, count, hop, close):
    for reverse in (False, True):
        order = list(range(count))[:: -1 if reverse else 1]
        total = get(order[0], reverse)
        for index in order[1:]:
            total = c_add(c_mul(hop, total), get(index, reverse))
        carry = c_mul(close, total)
        for index in order:
            put(index, reverse, carry)
            carry = c_add(c_mul(hop, carry), get(index, reverse))


def scan_rows(edge_ref, carry_ref, row_ref, section, pairs):
    hop, close = hop_of(row_ref, section)

    def get(block, reverse):
        first = 2 if reverse else 0
        lanes = slice(128 * (block % 2), 128 * (block % 2) + 128)
        return tuple(edge_ref[block // 2, first + part : first + part + 1, lanes] for part in range(2))

    def put(block, reverse, value):
        for part in range(2):
            first = (2 if reverse else 0) + part
            carry_ref[block, first : first + 1, :] = value[part]

    carries(get, put, 2 * pairs, hop, close)


def row_finish(section, operand_ref, factor_ref, grid_ref, edge_ref, pair):
    out = multiply(factor_ref, section, operand_ref)
    grid_ref[pair] = out[0:256]
    edge_ref[pair] = out[256:264]


def column_stage(section, operand_ref, weight_ref, carry_ref, grid_ref, pair):
    for half in range(2):
        lanes = slice(128 * half, 128 * half + 128)
        line = line_of(carry_ref, 2 * pair + half)
        for top in range(0, BLOCK, CHUNK):
            rows = slice(top, top + CHUNK)
            value = (grid_ref[pair, rows, lanes], grid_ref[pair, top + BLOCK : top + BLOCK + CHUNK, lanes])
            put_operand(operand_ref, 128 * half + top, *add_reach(weight_ref, section, rows, value, line))


def pack_edges(pair, ends, sums_ref):
    for half in range(2):
        sums_ref[2 * pair + half, 0:4, :] = ends[0:4, 128 * half : 128 * half + 128]


def pack_sums(section, out_ref, screen_ref, pair, row_ref, weight_ref, sums_ref):
    for half in range(2):
        block = 2 * pair + half
        lanes = lanes_of(pair, half)
        sums = [jnp.zeros((8, BLOCK), F32) for _ in range(10)]
        for top in range(0, BLOCK, 8):
            rows = slice(top, top + 8)
            screen = (screen_ref[0, rows, lanes], screen_ref[1, rows, lanes])
            value = c_mul(screen, (out_ref[0, rows, lanes], out_ref[1, rows, lanes]))
            weights = [(weight_ref[section, 2 * k, rows, :], weight_ref[section, 2 * k + 1, rows, :]) for k in range(2, 6)]
            terms = (c_mul(weights[0], value), c_mul(weights[1], value), screen, c_mul(weights[2], screen), c_mul(weights[3], screen))
            for k, term in enumerate(terms):
                sums[2 * k] = sums[2 * k] + term[0]
                sums[2 * k + 1] = sums[2 * k + 1] + term[1]
        lines = [jnp.sum(part, axis=0, keepdims=True) for part in sums]
        both = c_mul((row_line(row_ref, section, 12), row_line(row_ref, section, 13)), (lines[4], lines[5]))
        for k, line in enumerate(lines[0:4] + list(both) + lines[6:10]):
            sums_ref[block, 4 + k : 5 + k, :] = line
        sums_ref[block, 14:16, :] = jnp.zeros((2, BLOCK), F32)


def line_solve(section, back_ref, small_ref, line_ref, carry_ref, factor_ref, row_ref, blocks):
    small_ref[...] = jnp.zeros(small_ref.shape, F32)
    for block in range(blocks):
        for side in range(2):
            for part in range(2):
                row = 4 + 2 * side + part
                small_ref[8 * block + side : 8 * block + side + 1, 128 * part : 128 * part + 128] = back_ref[block, row : row + 1, :]
    high, low = split(small_ref[...])
    left = jnp.concatenate([high, high, low], axis=1)
    out = lax.dot_general(left, factor_ref[section], (((1,), (1,)), ((), ())), preferred_element_type=F32)
    line_ref[...] = out
    wide = (8, BLOCK)
    hop, close = (tuple(jnp.broadcast_to(part, wide) for part in pair) for pair in hop_of(row_ref, section))
    reach_left = tuple(row_ref[section, 8 * k : 8 * k + 8, :] for k in (4, 5))
    reach_right = tuple(row_ref[section, 8 * k : 8 * k + 8, :] for k in (6, 7))

    def get(block, reverse):
        first = 258 if reverse else 256
        rows = slice(8 * block, 8 * block + 8)
        return tuple(jnp.broadcast_to(line_ref[rows, first + part : first + part + 1], wide) for part in range(2))

    def put(block, reverse, value):
        rows = slice(8 * block, 8 * block + 8)
        add = c_mul(reach_right if reverse else reach_left, value)
        real = line_ref[rows, 0:128] + add[0]
        imaginary = line_ref[rows, 128:256] + add[1]
        if not reverse:
            line_ref[rows, 0:128] = real
            line_ref[rows, 128:256] = imaginary
        else:
            for side in range(2):
                carry_ref[block, 2 * side : 2 * side + 1, :] = real[side : side + 1]
                carry_ref[block, 2 * side + 1 : 2 * side + 2, :] = imaginary[side : side + 1]

    carries(get, put, blocks, hop, close)


def lanes_of(pair, half):
    return slice(256 * pair + 128 * half, 256 * pair + 128 * half + 128)


def wide_of(pair):
    return slice(256 * pair, 256 * pair + 256)


def steps(count, *bodies):
    for time in range(count + len(bodies) - 1):
        for depth, body in enumerate(bodies):
            if 0 <= time - depth < count:
                body(time - depth)


def first_kernel(pairs, field_any, own_any, other_any, factor_ref, weight_ref, row_ref, out_ref, sums_ref,
                 field_ref, label_ref, screen_ref, operand_ref, grid_ref, edge_ref, carry_ref, sems):
    mine = lax.axis_index("sect")

    def field_copy(pair):
        lanes = wide_of(pair)
        return pltpu.make_async_copy(field_any.at[mine, :, :, lanes], field_ref.at[:, :, lanes], sems.at[0, pair])

    def label_copy(source, pair):
        lanes = wide_of(pair)
        return pltpu.make_async_copy(source.at[0, :, lanes], label_ref.at[:, lanes], sems.at[1, pair])

    @pl.when(mine == 0)
    def _():
        for pair in range(pairs):
            label_copy(own_any, pair).start()
            field_copy(pair).start()

    @pl.when(mine != 0)
    def _():
        for pair in range(pairs):
            label_copy(other_any, pair).start()
            field_copy(pair).start()

    def stage(pair):
        if pair % LOADS == 0:
            for each in range(pair, pair + LOADS):
                field_copy(each).wait()
                label_copy(own_any, each).wait()
        for half in range(2):
            lanes = lanes_of(pair, half)
            for top in range(0, BLOCK, CHUNK):
                rows = slice(top, top + CHUNK)
                screen = screen_at(row_ref, 0, label_ref[rows, lanes])
                screen_ref[0, rows, lanes] = screen[0]
                screen_ref[1, rows, lanes] = screen[1]
                value = c_mul(screen, (field_ref[0, rows, lanes], field_ref[1, rows, lanes]))
                put_operand(operand_ref.at[pair % SLOTS], 128 * half + top, *value)

    steps(pairs, stage, lambda pair: row_finish(0, operand_ref.at[pair % SLOTS], factor_ref, grid_ref, edge_ref, pair))
    scan_rows(edge_ref, carry_ref, row_ref, 0, pairs)

    def leave(pair):
        value = multiply(factor_ref, 0, operand_ref.at[pair % SLOTS])
        out_ref[0, :, wide_of(pair)] = value[0:128]
        out_ref[1, :, wide_of(pair)] = value[128:256]
        pack_edges(pair, value[256:264], sums_ref)

    steps(
        pairs,
        lambda pair: column_stage(0, operand_ref.at[pair % SLOTS], weight_ref, carry_ref, grid_ref, pair),
        leave,
        lambda pair: pack_sums(0, out_ref, screen_ref, pair, row_ref, weight_ref, sums_ref),
    )


def middle_kernel(peers, section, held_ref, row_ref, back_ref):
    hop, close = hop_of(row_ref, section)

    def line(peer, row):
        return held_ref[peer, row : row + 1, :], held_ref[peer, row + 1 : row + 2, :]

    def keep(first):
        def put(peer, reverse, value):
            row = first + (2 if reverse else 0)
            back_ref[peer, row : row + 1, :] = value[0]
            back_ref[peer, row + 1 : row + 2, :] = value[1]

        return put

    carries(lambda peer, reverse: line(peer, 2 if reverse else 0), keep(0), peers, hop, close)

    def later(peer, reverse):
        left = (back_ref[peer, 0:1, :], back_ref[peer, 1:2, :])
        right = (back_ref[peer, 2:3, :], back_ref[peer, 3:4, :])
        if reverse:
            return c_add(line(peer, 6), c_add(c_mul(line(peer, 12), left), c_mul(line(peer, 8), right)))
        return c_add(line(peer, 4), c_add(c_mul(line(peer, 8), left), c_mul(line(peer, 10), right)))

    carries(later, keep(4), peers, hop, close)


def labels_of(section, own_ref, other_ref):
    mine = lax.axis_index("sect")
    return lambda rows, lanes: jnp.where(mine == section, own_ref[0, rows, lanes], other_ref[0, rows, lanes])


def take_in(section, pair, value_in, labels, weight_ref, back_ref, row_ref, operand_ref):
    for half in range(2):
        lanes = lanes_of(pair, half)
        line = line_of(back_ref, 2 * pair + half)
        for top in range(0, BLOCK, CHUNK):
            rows = slice(top, top + CHUNK)
            value = add_reach(weight_ref, section, rows, (value_in[0, rows, lanes], value_in[1, rows, lanes]), line)
            put_operand(operand_ref, 128 * half + top, *c_mul(screen_at(row_ref, section, labels(rows, lanes)), value))


def second_kernel(pairs, value_in, back_ref, own_ref, other_ref, zone_ref, factor_ref, weight_ref, row_ref, out_ref, sums_ref,
                  screen_ref, operand_ref, grid_ref, edge_ref, carry_ref, late_ref, small_ref, line_ref, inner_ref):
    labels = [labels_of(section, own_ref, other_ref) for section in range(2)]
    steps(
        pairs,
        lambda pair: take_in(0, pair, value_in, labels[0], weight_ref, back_ref, row_ref, operand_ref.at[pair % SLOTS]),
        lambda pair: row_finish(0, operand_ref.at[pair % SLOTS], factor_ref, grid_ref, edge_ref, pair),
    )
    line_solve(0, back_ref, small_ref, line_ref, late_ref, factor_ref, row_ref, 2 * pairs)
    scan_rows(edge_ref, carry_ref, row_ref, 0, pairs)

    def turn(pair):
        out = multiply(factor_ref, 0, operand_ref.at[pair % SLOTS])
        for half in range(2):
            inner = slice(128 * half, 128 * half + 128)
            lanes = lanes_of(pair, half)
            line = line_of(late_ref, 2 * pair + half)
            for top in range(0, BLOCK, CHUNK):
                rows = slice(top, top + CHUNK)
                value = (out[rows, inner], out[top + BLOCK : top + BLOCK + CHUNK, inner])
                value = add_reach(weight_ref, 0, rows, value, line)
                screen = screen_at(row_ref, 1, labels[1](rows, lanes))
                screen_ref[0, rows, lanes] = screen[0]
                screen_ref[1, rows, lanes] = screen[1]
                zones = zone_ref[rows, lanes]
                value = c_mul((pick(row_ref, 1, 2, zones), pick(row_ref, 1, 3, zones)), c_mul(screen, value))
                put_operand(inner_ref.at[pair % SLOTS], 128 * half + top, *value)

    steps(
        pairs,
        lambda pair: column_stage(0, operand_ref.at[pair % SLOTS], weight_ref, carry_ref, grid_ref, pair),
        turn,
        lambda pair: row_finish(1, inner_ref.at[pair % SLOTS], factor_ref, grid_ref, edge_ref, pair),
    )
    scan_rows(edge_ref, carry_ref, row_ref, 1, pairs)

    def leave(pair):
        value = multiply(factor_ref, 1, operand_ref.at[pair % SLOTS])
        out_ref[0, :, wide_of(pair)] = value[0:128]
        out_ref[1, :, wide_of(pair)] = value[128:256]
        pack_edges(pair, value[256:264], sums_ref)

    steps(
        pairs,
        lambda pair: column_stage(1, operand_ref.at[pair % SLOTS], weight_ref, carry_ref, grid_ref, pair),
        leave,
        lambda pair: pack_sums(1, out_ref, screen_ref, pair, row_ref, weight_ref, sums_ref),
    )


def third_kernel(pairs, value_in, back_ref, own_ref, other_ref, factor_ref, weight_ref, row_ref, out_ref,
                 operand_ref, grid_ref, edge_ref, carry_ref, late_ref, small_ref, line_ref):
    labels = labels_of(1, own_ref, other_ref)
    steps(
        pairs,
        lambda pair: take_in(1, pair, value_in, labels, weight_ref, back_ref, row_ref, operand_ref.at[pair % SLOTS]),
        lambda pair: row_finish(1, operand_ref.at[pair % SLOTS], factor_ref, grid_ref, edge_ref, pair),
    )
    line_solve(1, back_ref, small_ref, line_ref, late_ref, factor_ref, row_ref, 2 * pairs)
    scan_rows(edge_ref, carry_ref, row_ref, 1, pairs)

    def leave(pair):
        out = multiply(factor_ref, 1, operand_ref.at[pair % SLOTS])
        for half in range(2):
            inner = slice(128 * half, 128 * half + 128)
            lanes = lanes_of(pair, half)
            line = line_of(late_ref, 2 * pair + half)
            for top in range(0, BLOCK, CHUNK):
                rows = slice(top, top + CHUNK)
                value = (out[rows, inner], out[top + BLOCK : top + BLOCK + CHUNK, inner])
                value = add_reach(weight_ref, 1, rows, value, line)
                out_ref[0, 0, rows, lanes] = value[0]
                out_ref[0, 1, rows, lanes] = value[1]

    steps(pairs, lambda pair: column_stage(1, operand_ref.at[pair % SLOTS], weight_ref, carry_ref, grid_ref, pair), leave)


ANY = pl.BlockSpec(memory_space=pl.ANY)
VMEM = pl.BlockSpec(memory_space=pltpu.VMEM)
SMEM = pl.BlockSpec(memory_space=pltpu.SMEM)


def call(body, in_specs, out_shape, scratch=()):
    out_specs = jax.tree.map(lambda _: VMEM, out_shape)
    return pl.pallas_call(
        body,
        in_specs=in_specs,
        out_specs=out_specs,
        out_shape=out_shape,
        scratch_shapes=list(scratch),
        compiler_params=pltpu.CompilerParams(vmem_limit_bytes=VMEM_LIMIT),
        interpret=INTERPRET,
    )


def shape(*sizes, kind=F32):
    return jax.ShapeDtypeStruct(sizes, kind)


def kernels(peers, width):
    pairs = width // 256
    passing = [
        pltpu.VMEM((SLOTS, 256, 512), BF16),
        pltpu.VMEM((pairs, 256, 256), F32),
        pltpu.VMEM((pairs, 8, 256), F32),
        pltpu.VMEM((2 * pairs, 8, BLOCK), F32),
    ]
    small = [pltpu.VMEM((2 * pairs, 8, BLOCK), F32), pltpu.VMEM((16 * pairs, 256), F32), pltpu.VMEM((16 * pairs, 384), F32)]
    screen = pltpu.VMEM((2, BLOCK, width), F32)
    grids = (shape(2, BLOCK, width), shape(peers, 16, BLOCK))
    prepare = call(
        partial(prepare_kernel, width),
        [SMEM, SMEM, VMEM, VMEM],
        (shape(2, 384, 768, kind=BF16), shape(2, 12, BLOCK, BLOCK), shape(2, 8 * 14, BLOCK)),
        [pltpu.VMEM((8, BLOCK), F32)],
    )
    first = call(
        partial(first_kernel, pairs), [ANY] * 3 + [VMEM] * 3, grids,
        [pltpu.VMEM((2, BLOCK, width), F32), pltpu.VMEM((BLOCK, width), jnp.int32), screen]
        + passing
        + [pltpu.SemaphoreType.DMA((2, pairs))],
    )
    middle = [call(partial(middle_kernel, peers, section), [VMEM, VMEM], shape(peers, 8, BLOCK)) for section in range(2)]
    second = call(partial(second_kernel, pairs), [VMEM] * 8, grids, [screen] + passing + small + passing[:1])
    third = call(partial(third_kernel, pairs), [VMEM] * 7, shape(1, 2, BLOCK, width), passing + small)
    return prepare, first, middle, second, third


def stay(value):
    return value if INTERPRET else pltpu.with_memory_space_constraint(value, pltpu.HBM)


def fast_shards(fields, region_ids, index_offsets, step_lengths, wave_numbers, zone_ids, zone_phases):
    prepare, first, middle, second, third = kernels(lax.axis_size("slab"), fields.shape[-1])
    other = lax.ppermute(region_ids, "sect", [(0, 1), (1, 0)])
    factor, weights, row = prepare(stay(wave_numbers), stay(step_lengths), stay(index_offsets), stay(zone_phases))

    def exchange(sums, section):
        held = lax.all_to_all(sums, "slab", 0, 0, tiled=True)
        return lax.all_to_all(middle[section](held, row), "slab", 0, 0, tiled=True)

    value, sums = first(stay(fields), stay(region_ids), other, factor, weights, row)
    back = exchange(sums, 0)
    value, sums = second(value, back, region_ids, other, zone_ids, factor, weights, row)
    back = exchange(sums, 1)
    return third(value, back, region_ids, other, factor, weights, row)


def choose(fields, *others):
    rows, width = fields.shape[-2:]
    if rows == BLOCK and width == BLOCK * lax.axis_size("slab") and lax.axis_size("sect") == 2:
        return fast_shards(fields, *others)
    return shards(fields, *others)


def solution(mesh):
    return jax.shard_map(
        choose,
        mesh=mesh,
        in_specs=(
            P(None, None, "slab", None),
            P("sect", "slab", None),
            P(),
            P(),
            P(),
            P("slab", None),
            P(),
        ),
        out_specs=P("sect", None, "slab", None),
        check_vma=False,
    )
```

time: 108 us -> 76.6 us (0.71)
  Pallas kernels: 52.4 us -> 29 us
  blocking collectives: 51.4 us -> 46.7 us
  local copies, waits for them, and re-layouts: 3.49 us -> 0.01 us
    pallas_call x6, Pallas kernels: 52.4 us -> 29 us  [the longest x1 11.6 us: fast_shards(): second(value, back, region_ids, other, zone_ids, factor, weights, row)]
    all_to_all x2, blocking collectives: 23.4 us -> 20.6 us  [exchange(): return lax.all_to_all(middle[section](held, row), 'slab', 0, 0, tiled=True)]
    pad x2 -> x0, local copies, waits for them, and re-layouts: 2.52 us -> none  [padded(): return jnp.pad(table, ((0, 0), (0, BLOCK - table.shape[1])))]
    all_to_all x2, blocking collectives: 28.1 us -> 26.1 us  [exchange(): held = lax.all_to_all(sums, 'slab', 0, 0, tiled=True)]
  transfers between devices with their start and end apart: 1 -> 1, of which waited for: 0 -> 0; matrix products, arithmetic and copies ran while one was open for 2% -> 0% of each run, Pallas kernels for 3% -> 3%
where the time goes in v3:
time: 76.6 us; the launch traced here: 76.3 us
  blocking collectives  46.7 us (61%)
  Pallas kernels  29 us (38%)
    all_to_all x2, blocking collectives, exchange(): held = lax.all_to_all(sums, 'slab', 0, 0, tiled=True)  26.1 us
    all_to_all x2, blocking collectives, exchange(): return lax.all_to_all(middle[section](held, row), 'slab', 0, 0, tiled=True)  20.6 us
    pallas_call x1, Pallas kernels, fast_shards(): second(value, back, region_ids, other, zone_ids, factor, weights, row)  11.6 us
    pallas_call x1, Pallas kernels, fast_shards(): first(stay(fields), stay(region_ids), other, factor, weights, row)  7.9 us
    pallas_call x1, Pallas kernels, fast_shards(): return third(value, back, region_ids, other, factor, weights, row)  6.33 us
    pallas_call x1, Pallas kernels, fast_shards(): prepare(stay(wave_numbers), stay(step_lengths), stay(index_offsets), stay...  2.59 us
  transfers between devices with their start and end apart: 1, of which 0 were waited for; matrix products, arithmetic and copies ran while one was open for 0% of the time, Pallas kernels for 3%

profile of v3, /device:TPU:0, one launch (start us, length us, event | category | flops | bytes accessed | tf_op | source)
XLA Modules:
  0.0 76.3 jit_solution(5765592389445890996)
XLA Ops:
  0.0 0.5 collective-permute-start
  0.5 2.6 %shard_map.73 = (bf16[2,384,768]{2,1,0:T(8,128)(2,1)S(1)}, f32[2,12,128,128]{3,2,1,0:T(8,128)S(1)}, f32[2,112,128]{2,1,0:T(8,128)S(1)}) custom-call(f32[2]{0:T(128)} %number_ref.1, f32[2]{0:T(128)} %length_ref.1, f32[2,16]{1,0:T(2,128)} %offset_ref.1, f32[2,32]{1,0:T(2,128)} %zone_ref.2), custom_call_target="tpu_custom_call" | custom-call | tf_op jit(solution)/shard_map/pallas_call | solution.py:695
  3.0 0.0 collective-permute-done.other_any.other_ref
  3.1 0.0 copy-start
  3.1 0.0 copy-start.1
  3.1 7.9 %shard_map.74 = (f32[2,128,2048]{2,1,0:T(8,128)S(1)}, f32[16,16,128]{2,1,0:T(8,128)S(1)}) custom-call(f32[2,2,128,2048]{3,2,1,0:T(8,128)} %field_any.1, s32[1,128,2048]{2,1,0:T(8,128)} %own_ref.3, s32[1,128,2048]{2,1,0:T(8,128)S(1)} %collective-permute-done.other_any.other_ref, bf16[2,384,768]{2,1,0:T(8,128)(2,1)S(1)} %get-tuple-element.12.factor_ref, ...), custom_call_target="tpu_custom_call" | custom-call | tf_op jit(solution)/shard_map/pallas_call | solution.py:701
  11.0 15.7 %all_to_all.20.held_ref = f32[16,16,128]{2,1,0:T(8,128)S(1)} all-to-all(f32[16,16,128]{2,1,0:T(8,128)S(1)} %get-tuple-element.16), channel_id=1, replica_groups=mesh['slab'=16,'sect'=2] {'slab'}, dimensions={0} | all-to-all | bytes 262144 | tf_op jit(solution)/shard_map/all_to_all | solution.py:698
  26.7 0.3 shard_map.75
  27.0 10.5 %all_to_all.21.back_ref = f32[16,8,128]{2,1,0:T(8,128)S(1)} all-to-all(f32[16,8,128]{2,1,0:T(8,128)S(1)} %shard_map.75), channel_id=1, replica_groups=mesh['slab'=16,'sect'=2] {'slab'}, dimensions={0} | all-to-all | bytes 131072 | tf_op jit(solution)/shard_map/all_to_all | solution.py:699
  37.5 0.0 copy-done
  37.6 0.0 copy-done.1
  37.6 11.6 %shard_map.76 = (f32[2,128,2048]{2,1,0:T(8,128)S(1)}, f32[16,16,128]{2,1,0:T(8,128)S(1)}) custom-call(f32[2,128,2048]{2,1,0:T(8,128)S(1)} %get-tuple-element.15.value_in, f32[16,8,128]{2,1,0:T(8,128)S(1)} %all_to_all.21.back_ref, s32[1,128,2048]{2,1,0:T(8,128)S(1)} %copy-done, s32[1,128,2048]{2,1,0:T(8,128)S(1)} %collective-permute-done.other_any.other_ref, ...), custom_call_target="tpu_custom_call" | custom-call | tf_op jit(solution)/shard_map/pallas_call | solution.py:703
  49.2 10.4 %all_to_all.22.held_ref = f32[16,16,128]{2,1,0:T(8,128)S(1)} all-to-all(f32[16,16,128]{2,1,0:T(8,128)S(1)} %get-tuple-element.18), channel_id=1, replica_groups=mesh['slab'=16,'sect'=2] {'slab'}, dimensions={0} | all-to-all | bytes 262144 | tf_op jit(solution)/shard_map/all_to_all | solution.py:698
  59.5 0.3 shard_map.77
  59.9 10.1 %all_to_all.23.back_ref = f32[16,8,128]{2,1,0:T(8,128)S(1)} all-to-all(f32[16,8,128]{2,1,0:T(8,128)S(1)} %shard_map.77), channel_id=1, replica_groups=mesh['slab'=16,'sect'=2] {'slab'}, dimensions={0} | all-to-all | bytes 131072 | tf_op jit(solution)/shard_map/all_to_all | solution.py:699
  70.0 6.3 %shard_map.78 = f32[1,2,128,2048]{3,2,1,0:T(8,128)} custom-call(f32[2,128,2048]{2,1,0:T(8,128)S(1)} %get-tuple-element.17.value_in, f32[16,8,128]{2,1,0:T(8,128)S(1)} %all_to_all.23.back_ref, s32[1,128,2048]{2,1,0:T(8,128)S(1)} %copy-done, s32[1,128,2048]{2,1,0:T(8,128)S(1)} %collective-permute-done.other_any.other_ref, ...), custom_call_target="tpu_custom_call" | custom-call | tf_op jit(solution)/shard_map/pallas_call | solution.py:705
Async XLA Ops:
  0.0 3.1 %collective-permute-start = (s32[1,128,2048]{2,1,0:T(8,128)}, s32[1,128,2048]{2,1,0:T(8,128)S(1)}, u32[]{:S(2)}, u32[]{:S(2)}) collective-permute-start(s32[1,128,2048]{2,1,0:T(8,128)} %own_ref.3), channel_id=1, source_target_pairs={{0,1},{1,0},{2,3},{3,2},{4,5},{5,4},{6,7},{7,6},{8,9},{9,8},{10,11... | collective-permute-start | bytes 3145736 | tf_op jit(solution)/shard_map/ppermute | solution.py:694
  3.1 34.5 %copy-start = (s32[1,128,2048]{2,1,0:T(8,128)S(1)}, s32[1,128,2048]{2,1,0:T(8,128)}, u32[]{:S(2)}) copy-start(s32[1,128,2048]{2,1,0:T(8,128)} %own_ref.3) | copy-start | bytes 3145732
  3.1 34.5 %copy-start.1 = (s32[128,2048]{1,0:T(8,128)S(1)}, s32[128,2048]{1,0:T(8,128)}, u32[]{:S(2)}) copy-start(s32[128,2048]{1,0:T(8,128)} %zone_ref.3) | copy-start | bytes 3145732

commit v4 on v3

--- a/solution.py
+++ b/solution.py
@@ -183,7 +183,6 @@
 F32 = jnp.float32
 BF16 = jnp.bfloat16
 LHS_ROWS = 272
-LOADS = 1
 SLOTS = 2
 
 CHUNK = 32
@@ -210,8 +209,15 @@
     return tuple(jnp.broadcast_to(part[0:1, 0:1], shape) for part in pair)
 
 
-def prepare_kernel(total, number_ref, length_ref, offset_ref, zone_ref, factor_ref, weight_ref, row_ref, pad_ref):
+def prepare_kernel(total, number_ref, length_ref, offset_ref, zone_ref, field_any, label_any,
+                   factor_ref, weight_ref, row_ref, field_ref, label_ref, pad_ref, sems):
     mine = lax.axis_index("sect")
+    copies = [
+        pltpu.make_async_copy(field_any.at[mine], field_ref, sems.at[0]),
+        pltpu.make_async_copy(label_any, label_ref, sems.at[1]),
+    ]
+    for copy in copies:
+        copy.start()
     number = tile_of(number_ref[mine])
     tall = (BLOCK, BLOCK)
     place = lax.broadcasted_iota(jnp.int32, tall, 0)
@@ -288,6 +294,8 @@
         for index, table in enumerate(tables):
             weight_ref[section, 2 * index] = table[0]
             weight_ref[section, 2 * index + 1] = table[1]
+    for copy in copies:
+        copy.wait()
 
 
 def split(value):
@@ -460,40 +468,16 @@
                 body(time - depth)
 
 
-def first_kernel(pairs, field_any, own_any, other_any, factor_ref, weight_ref, row_ref, out_ref, sums_ref,
-                 field_ref, label_ref, screen_ref, operand_ref, grid_ref, edge_ref, carry_ref, sems):
-    mine = lax.axis_index("sect")
-
-    def field_copy(pair):
-        lanes = wide_of(pair)
-        return pltpu.make_async_copy(field_any.at[mine, :, :, lanes], field_ref.at[:, :, lanes], sems.at[0, pair])
-
-    def label_copy(source, pair):
-        lanes = wide_of(pair)
-        return pltpu.make_async_copy(source.at[0, :, lanes], label_ref.at[:, lanes], sems.at[1, pair])
-
-    @pl.when(mine == 0)
-    def _():
-        for pair in range(pairs):
-            label_copy(own_any, pair).start()
-            field_copy(pair).start()
-
-    @pl.when(mine != 0)
-    def _():
-        for pair in range(pairs):
-            label_copy(other_any, pair).start()
-            field_copy(pair).start()
+def first_kernel(pairs, field_ref, own_ref, other_ref, factor_ref, weight_ref, row_ref, out_ref, sums_ref, screen_ref,
+                 operand_ref, grid_ref, edge_ref, carry_ref):
+    labels = labels_of(0, own_ref, other_ref)
 
     def stage(pair):
-        if pair % LOADS == 0:
-            for each in range(pair, pair + LOADS):
-                field_copy(each).wait()
-                label_copy(own_any, each).wait()
         for half in range(2):
             lanes = lanes_of(pair, half)
             for top in range(0, BLOCK, CHUNK):
                 rows = slice(top, top + CHUNK)
-                screen = screen_at(row_ref, 0, label_ref[rows, lanes])
+                screen = screen_at(row_ref, 0, labels(rows, lanes))
                 screen_ref[0, rows, lanes] = screen[0]
                 screen_ref[1, rows, lanes] = screen[1]
                 value = c_mul(screen, (field_ref[0, rows, lanes], field_ref[1, rows, lanes]))
@@ -547,22 +531,22 @@
     return lambda rows, lanes: jnp.where(mine == section, own_ref[0, rows, lanes], other_ref[0, rows, lanes])
 
 
-def take_in(section, pair, value_in, labels, weight_ref, back_ref, row_ref, operand_ref):
+def take_in(section, pair, value_in, screen_in, weight_ref, back_ref, operand_ref):
     for half in range(2):
         lanes = lanes_of(pair, half)
         line = line_of(back_ref, 2 * pair + half)
         for top in range(0, BLOCK, CHUNK):
             rows = slice(top, top + CHUNK)
             value = add_reach(weight_ref, section, rows, (value_in[0, rows, lanes], value_in[1, rows, lanes]), line)
-            put_operand(operand_ref, 128 * half + top, *c_mul(screen_at(row_ref, section, labels(rows, lanes)), value))
-
-
-def second_kernel(pairs, value_in, back_ref, own_ref, other_ref, zone_ref, factor_ref, weight_ref, row_ref, out_ref, sums_ref,
-                  screen_ref, operand_ref, grid_ref, edge_ref, carry_ref, late_ref, small_ref, line_ref, inner_ref):
-    labels = [labels_of(section, own_ref, other_ref) for section in range(2)]
+            put_operand(operand_ref, 128 * half + top, *c_mul((screen_in[0, rows, lanes], screen_in[1, rows, lanes]), value))
+
+
+def second_kernel(pairs, value_in, back_ref, screen_in, own_ref, other_ref, zone_ref, factor_ref, weight_ref, row_ref,
+                  out_ref, sums_ref, screen_ref, operand_ref, grid_ref, edge_ref, carry_ref, late_ref, small_ref, line_ref, inner_ref):
+    labels = labels_of(1, own_ref, other_ref)
     steps(
         pairs,
-        lambda pair: take_in(0, pair, value_in, labels[0], weight_ref, back_ref, row_ref, operand_ref.at[pair % SLOTS]),
+        lambda pair: take_in(0, pair, value_in, screen_in, weight_ref, back_ref, operand_ref.at[pair % SLOTS]),
         lambda pair: row_finish(0, operand_ref.at[pair % SLOTS], factor_ref, grid_ref, edge_ref, pair),
     )
     line_solve(0, back_ref, small_ref, line_ref, late_ref, factor_ref, row_ref, 2 * pairs)
@@ -578,7 +562,7 @@
                 rows = slice(top, top + CHUNK)
                 value = (out[rows, inner], out[top + BLOCK : top + BLOCK + CHUNK, inner])
                 value = add_reach(weight_ref, 0, rows, value, line)
-                screen = screen_at(row_ref, 1, labels[1](rows, lanes))
+                screen = screen_at(row_ref, 1, labels(rows, lanes))
                 screen_ref[0, rows, lanes] = screen[0]
                 screen_ref[1, rows, lanes] = screen[1]
                 zones = zone_ref[rows, lanes]
@@ -607,12 +591,11 @@
     )
 
 
-def third_kernel(pairs, value_in, back_ref, own_ref, other_ref, factor_ref, weight_ref, row_ref, out_ref,
+def third_kernel(pairs, value_in, back_ref, screen_in, factor_ref, weight_ref, row_ref, out_ref,
                  operand_ref, grid_ref, edge_ref, carry_ref, late_ref, small_ref, line_ref):
-    labels = labels_of(1, own_ref, other_ref)
     steps(
         pairs,
-        lambda pair: take_in(1, pair, value_in, labels, weight_ref, back_ref, row_ref, operand_ref.at[pair % SLOTS]),
+        lambda pair: take_in(1, pair, value_in, screen_in, weight_ref, back_ref, operand_ref.at[pair % SLOTS]),
         lambda pair: row_finish(1, operand_ref.at[pair % SLOTS], factor_ref, grid_ref, edge_ref, pair),
     )
     line_solve(1, back_ref, small_ref, line_ref, late_ref, factor_ref, row_ref, 2 * pairs)
@@ -665,23 +648,21 @@
         pltpu.VMEM((2 * pairs, 8, BLOCK), F32),
     ]
     small = [pltpu.VMEM((2 * pairs, 8, BLOCK), F32), pltpu.VMEM((16 * pairs, 256), F32), pltpu.VMEM((16 * pairs, 384), F32)]
-    screen = pltpu.VMEM((2, BLOCK, width), F32)
-    grids = (shape(2, BLOCK, width), shape(peers, 16, BLOCK))
+    grid = shape(2, BLOCK, width)
+    grids = (grid, shape(peers, 16, BLOCK), grid)
     prepare = call(
         partial(prepare_kernel, width),
-        [SMEM, SMEM, VMEM, VMEM],
-        (shape(2, 384, 768, kind=BF16), shape(2, 12, BLOCK, BLOCK), shape(2, 8 * 14, BLOCK)),
-        [pltpu.VMEM((8, BLOCK), F32)],
-    )
-    first = call(
-        partial(first_kernel, pairs), [ANY] * 3 + [VMEM] * 3, grids,
-        [pltpu.VMEM((2, BLOCK, width), F32), pltpu.VMEM((BLOCK, width), jnp.int32), screen]
-        + passing
-        + [pltpu.SemaphoreType.DMA((2, pairs))],
-    )
+        [SMEM, SMEM, VMEM, VMEM, ANY, ANY],
+        (
+            shape(2, 384, 768, kind=BF16), shape(2, 12, BLOCK, BLOCK), shape(2, 8 * 14, BLOCK),
+            grid, shape(1, BLOCK, width, kind=jnp.int32),
+        ),
+        [pltpu.VMEM((8, BLOCK), F32), pltpu.SemaphoreType.DMA((2,))],
+    )
+    first = call(partial(first_kernel, pairs), [VMEM] * 6, grids, passing)
     middle = [call(partial(middle_kernel, peers, section), [VMEM, VMEM], shape(peers, 8, BLOCK)) for section in range(2)]
-    second = call(partial(second_kernel, pairs), [VMEM] * 8, grids, [screen] + passing + small + passing[:1])
-    third = call(partial(third_kernel, pairs), [VMEM] * 7, shape(1, 2, BLOCK, width), passing + small)
+    second = call(partial(second_kernel, pairs), [VMEM] * 9, grids, passing + small + passing[:1])
+    third = call(partial(third_kernel, pairs), [VMEM] * 6, shape(1, 2, BLOCK, width), passing + small)
     return prepare, first, middle, second, third
 
 
@@ -692,17 +673,18 @@
 def fast_shards(fields, region_ids, index_offsets, step_lengths, wave_numbers, zone_ids, zone_phases):
     prepare, first, middle, second, third = kernels(lax.axis_size("slab"), fields.shape[-1])
     other = lax.ppermute(region_ids, "sect", [(0, 1), (1, 0)])
-    factor, weights, row = prepare(stay(wave_numbers), stay(step_lengths), stay(index_offsets), stay(zone_phases))
+    small = [stay(table) for table in (wave_numbers, step_lengths, index_offsets, zone_phases)]
+    factor, weights, row, field, own = prepare(*small, stay(fields), stay(region_ids))
 
     def exchange(sums, section):
         held = lax.all_to_all(sums, "slab", 0, 0, tiled=True)
         return lax.all_to_all(middle[section](held, row), "slab", 0, 0, tiled=True)
 
-    value, sums = first(stay(fields), stay(region_ids), other, factor, weights, row)
+    value, sums, screen = first(field, own, other, factor, weights, row)
     back = exchange(sums, 0)
-    value, sums = second(value, back, region_ids, other, zone_ids, factor, weights, row)
+    value, sums, screen = second(value, back, screen, own, other, zone_ids, factor, weights, row)
     back = exchange(sums, 1)
-    return third(value, back, region_ids, other, factor, weights, row)
+    return third(value, back, screen, factor, weights, row)
 
 
 def choose(fields, *others):

time: 76.6 us -> 74.2 us (0.969)
  Pallas kernels: 29 us -> 26.6 us
    pallas_call x4, Pallas kernels: 28.4 us -> 25.9 us  [the longest x1 11.4 us: fast_shards(): second(value, back, screen, own, other, zone_ids, factor, weights, row)]
  transfers between devices with their start and end apart: 1 -> 1, of which waited for: 0 -> 0; matrix products, arithmetic and copies ran while one was open for 0% -> 0% of each run, Pallas kernels for 3% -> 4%
where the time goes in v4:
time: 74.2 us; the launch traced here: 73.9 us
  blocking collectives  46.8 us (63%)
  Pallas kernels  26.6 us (36%)
    all_to_all x2, blocking collectives, exchange(): held = lax.all_to_all(sums, 'slab', 0, 0, tiled=True)  26.2 us
    all_to_all x2, blocking collectives, exchange(): return lax.all_to_all(middle[section](held, row), 'slab', 0, 0, tiled=True)  20.6 us
    pallas_call x1, Pallas kernels, fast_shards(): second(value, back, screen, own, other, zone_ids, factor, weights, row)  11.4 us
    pallas_call x1, Pallas kernels, fast_shards(): return third(value, back, screen, factor, weights, row)  6.5 us
    pallas_call x1, Pallas kernels, fast_shards(): value, sums, screen = first(field, own, other, factor, weights, row)  5.49 us
    pallas_call x1, Pallas kernels, fast_shards(): prepare(*small, stay(fields), stay(region_ids))  2.61 us
  transfers between devices with their start and end apart: 1, of which 0 were waited for; matrix products, arithmetic and copies ran while one was open for 0% of the time, Pallas kernels for 4%

profile of v4, /device:TPU:0, one launch (start us, length us, event | category | flops | bytes accessed | tf_op | source)
XLA Modules:
  0.0 73.9 jit_solution(11699853445563327465)
XLA Ops:
  0.0 0.5 collective-permute-start
  0.5 2.6 %shard_map.73 = (bf16[2,384,768]{2,1,0:T(8,128)(2,1)S(1)}, f32[2,12,128,128]{3,2,1,0:T(8,128)S(1)}, f32[2,112,128]{2,1,0:T(8,128)S(1)}, f32[2,128,2048]{2,1,0:T(8,128)S(1)}, s32[1,128,2048]{2,1,0:T(8,128)S(1)}) custom-call(f32[2]{0:T(128)} %number_ref.1, f32[2]{0:T(128)} %length_ref.1, f32[2,16]{1,0:T(2,128)} %offset_ref.1, f32[2,32]{1,0:T(2,128)} %zone_ref.2, ...), custom_call_target="tpu_custom_call" | custom-call | tf_op jit(solution)/shard_map/pallas_call | solution.py:677
  3.1 0.0 collective-permute-done.other_ref
  3.1 0.0 copy-start
  3.1 5.5 %shard_map.74 = (f32[2,128,2048]{2,1,0:T(8,128)S(1)}, f32[16,16,128]{2,1,0:T(8,128)S(1)}, f32[2,128,2048]{2,1,0:T(8,128)S(1)}) custom-call(f32[2,128,2048]{2,1,0:T(8,128)S(1)} %get-tuple-element.16.field_ref, s32[1,128,2048]{2,1,0:T(8,128)S(1)} %get-tuple-element.17.own_ref, s32[1,128,2048]{2,1,0:T(8,128)S(1)} %collective-permute-done.other_ref, ...), custom_call_target="tpu_custom_call" | custom-call | tf_op jit(solution)/shard_map/pallas_call | solution.py:683
  8.6 15.8 %all_to_all.20.held_ref = f32[16,16,128]{2,1,0:T(8,128)S(1)} all-to-all(f32[16,16,128]{2,1,0:T(8,128)S(1)} %get-tuple-element.22), channel_id=1, replica_groups=mesh['slab'=16,'sect'=2] {'slab'}, dimensions={0} | all-to-all | bytes 262144 | tf_op jit(solution)/shard_map/all_to_all | solution.py:680
  24.4 0.3 shard_map.75
  24.7 10.5 %all_to_all.21.back_ref = f32[16,8,128]{2,1,0:T(8,128)S(1)} all-to-all(f32[16,8,128]{2,1,0:T(8,128)S(1)} %shard_map.75), channel_id=1, replica_groups=mesh['slab'=16,'sect'=2] {'slab'}, dimensions={0} | all-to-all | bytes 131072 | tf_op jit(solution)/shard_map/all_to_all | solution.py:681
  35.2 0.0 copy-done
  35.2 11.4 %shard_map.76 = (f32[2,128,2048]{2,1,0:T(8,128)S(1)}, f32[16,16,128]{2,1,0:T(8,128)S(1)}, f32[2,128,2048]{2,1,0:T(8,128)S(1)}) custom-call(f32[2,128,2048]{2,1,0:T(8,128)S(1)} %get-tuple-element.21.value_in, f32[16,8,128]{2,1,0:T(8,128)S(1)} %all_to_all.21.back_ref, f32[2,128,2048]{2,1,0:T(8,128)S(1)} %get-tuple-element.23.screen_in, ...), custom_call_target="tpu_custom_call" | custom-call | tf_op jit(solution)/shard_map/pallas_call | solution.py:685
  46.5 10.4 %all_to_all.22.held_ref = f32[16,16,128]{2,1,0:T(8,128)S(1)} all-to-all(f32[16,16,128]{2,1,0:T(8,128)S(1)} %get-tuple-element.25), channel_id=1, replica_groups=mesh['slab'=16,'sect'=2] {'slab'}, dimensions={0} | all-to-all | bytes 262144 | tf_op jit(solution)/shard_map/all_to_all | solution.py:680
  56.9 0.3 shard_map.77
  57.3 10.1 %all_to_all.23.back_ref = f32[16,8,128]{2,1,0:T(8,128)S(1)} all-to-all(f32[16,8,128]{2,1,0:T(8,128)S(1)} %shard_map.77), channel_id=1, replica_groups=mesh['slab'=16,'sect'=2] {'slab'}, dimensions={0} | all-to-all | bytes 131072 | tf_op jit(solution)/shard_map/all_to_all | solution.py:681
  67.4 6.5 %shard_map.78 = f32[1,2,128,2048]{3,2,1,0:T(8,128)} custom-call(f32[2,128,2048]{2,1,0:T(8,128)S(1)} %get-tuple-element.24.value_in, f32[16,8,128]{2,1,0:T(8,128)S(1)} %all_to_all.23.back_ref, f32[2,128,2048]{2,1,0:T(8,128)S(1)} %get-tuple-element.26.screen_in, bf16[2,384,768]{2,1,0:T(8,128)(2,1)S(1)} %get-tuple-element.18.factor_ref, ...), custom_call_target="tpu_custom_call" | custom-call | tf_op jit(solution)/shard_map/pallas_call | solution.py:687
Async XLA Ops:
  0.0 3.1 %collective-permute-start = (s32[1,128,2048]{2,1,0:T(8,128)}, s32[1,128,2048]{2,1,0:T(8,128)S(1)}, u32[]{:S(2)}, u32[]{:S(2)}) collective-permute-start(s32[1,128,2048]{2,1,0:T(8,128)} %label_any.1), channel_id=1, source_target_pairs={{0,1},{1,0},{2,3},{3,2},{4,5},{5,4},{6,7},{7,6},{8,9},{9,8},{10,11... | collective-permute-start | bytes 3145736 | tf_op jit(solution)/shard_map/ppermute | solution.py:675
  3.1 32.1 %copy-start = (s32[128,2048]{1,0:T(8,128)S(1)}, s32[128,2048]{1,0:T(8,128)}, u32[]{:S(2)}) copy-start(s32[128,2048]{1,0:T(8,128)} %zone_ref.3) | copy-start | bytes 3145732

commit v5 on v4

--- a/solution.py
+++ b/solution.py
@@ -319,9 +319,12 @@
     return lax.dot_general(factor_ref[section, 0:LHS_ROWS, :], right, (((1,), (1,)), ((), ())), preferred_element_type=F32)
 
 
-def add_reach(weight_ref, section, rows, value, line):
-    high = (weight_ref[section, 0, rows, :], weight_ref[section, 1, rows, :])
-    low = (weight_ref[section, 2, rows, :], weight_ref[section, 3, rows, :])
+def reach_of(weight_ref, section, rows):
+    return [weight_ref[section, index, rows, :] for index in range(4)]
+
+
+def add_reach(table, value, line):
+    high, low = table[0:2], table[2:4]
     return c_add(value, c_add(c_mul(high, (line[0], line[1])), c_mul(low, (line[2], line[3]))))
 
 
@@ -381,13 +384,14 @@
 
 
 def column_stage(section, operand_ref, weight_ref, carry_ref, grid_ref, pair):
-    for half in range(2):
-        lanes = slice(128 * half, 128 * half + 128)
-        line = line_of(carry_ref, 2 * pair + half)
-        for top in range(0, BLOCK, CHUNK):
-            rows = slice(top, top + CHUNK)
+    lines = [line_of(carry_ref, 2 * pair + half) for half in range(2)]
+    for top in range(0, BLOCK, CHUNK):
+        rows = slice(top, top + CHUNK)
+        table = reach_of(weight_ref, section, rows)
+        for half in range(2):
+            lanes = slice(128 * half, 128 * half + 128)
             value = (grid_ref[pair, rows, lanes], grid_ref[pair, top + BLOCK : top + BLOCK + CHUNK, lanes])
-            put_operand(operand_ref, 128 * half + top, *add_reach(weight_ref, section, rows, value, line))
+            put_operand(operand_ref, 128 * half + top, *add_reach(table, value, lines[half]))
 
 
 def pack_edges(pair, ends, sums_ref):
@@ -532,12 +536,13 @@
 
 
 def take_in(section, pair, value_in, screen_in, weight_ref, back_ref, operand_ref):
-    for half in range(2):
-        lanes = lanes_of(pair, half)
-        line = line_of(back_ref, 2 * pair + half)
-        for top in range(0, BLOCK, CHUNK):
-            rows = slice(top, top + CHUNK)
-            value = add_reach(weight_ref, section, rows, (value_in[0, rows, lanes], value_in[1, rows, lanes]), line)
+    lines = [line_of(back_ref, 2 * pair + half) for half in range(2)]
+    for top in range(0, BLOCK, CHUNK):
+        rows = slice(top, top + CHUNK)
+        table = reach_of(weight_ref, section, rows)
+        for half in range(2):
+            lanes = lanes_of(pair, half)
+            value = add_reach(table, (value_in[0, rows, lanes], value_in[1, rows, lanes]), lines[half])
             put_operand(operand_ref, 128 * half + top, *c_mul((screen_in[0, rows, lanes], screen_in[1, rows, lanes]), value))
 
 
@@ -554,14 +559,15 @@
 
     def turn(pair):
         out = multiply(factor_ref, 0, operand_ref.at[pair % SLOTS])
-        for half in range(2):
-            inner = slice(128 * half, 128 * half + 128)
-            lanes = lanes_of(pair, half)
-            line = line_of(late_ref, 2 * pair + half)
-            for top in range(0, BLOCK, CHUNK):
-                rows = slice(top, top + CHUNK)
+        lines = [line_of(late_ref, 2 * pair + half) for half in range(2)]
+        for top in range(0, BLOCK, CHUNK):
+            rows = slice(top, top + CHUNK)
+            table = reach_of(weight_ref, 0, rows)
+            for half in range(2):
+                inner = slice(128 * half, 128 * half + 128)
+                lanes = lanes_of(pair, half)
                 value = (out[rows, inner], out[top + BLOCK : top + BLOCK + CHUNK, inner])
-                value = add_reach(weight_ref, 0, rows, value, line)
+                value = add_reach(table, value, lines[half])
                 screen = screen_at(row_ref, 1, labels(rows, lanes))
                 screen_ref[0, rows, lanes] = screen[0]
                 screen_ref[1, rows, lanes] = screen[1]
@@ -591,8 +597,12 @@
     )
 
 
-def third_kernel(pairs, value_in, back_ref, screen_in, factor_ref, weight_ref, row_ref, out_ref,
-                 operand_ref, grid_ref, edge_ref, carry_ref, late_ref, small_ref, line_ref):
+def third_kernel(pairs, value_in, back_ref, screen_in, factor_ref, weight_ref, row_ref, out_any,
+                 operand_ref, grid_ref, edge_ref, carry_ref, late_ref, small_ref, line_ref, out_ref, sems):
+    def write(pair):
+        wide = wide_of(pair)
+        return pltpu.make_async_copy(out_ref.at[:, :, wide], out_any.at[0, :, :, wide], sems.at[pair])
+
     steps(
         pairs,
         lambda pair: take_in(1, pair, value_in, screen_in, weight_ref, back_ref, operand_ref.at[pair % SLOTS]),
@@ -603,18 +613,22 @@
 
     def leave(pair):
         out = multiply(factor_ref, 1, operand_ref.at[pair % SLOTS])
-        for half in range(2):
-            inner = slice(128 * half, 128 * half + 128)
-            lanes = lanes_of(pair, half)
-            line = line_of(late_ref, 2 * pair + half)
-            for top in range(0, BLOCK, CHUNK):
-                rows = slice(top, top + CHUNK)
+        lines = [line_of(late_ref, 2 * pair + half) for half in range(2)]
+        for top in range(0, BLOCK, CHUNK):
+            rows = slice(top, top + CHUNK)
+            table = reach_of(weight_ref, 1, rows)
+            for half in range(2):
+                inner = slice(128 * half, 128 * half + 128)
+                lanes = lanes_of(pair, half)
                 value = (out[rows, inner], out[top + BLOCK : top + BLOCK + CHUNK, inner])
-                value = add_reach(weight_ref, 1, rows, value, line)
-                out_ref[0, 0, rows, lanes] = value[0]
-                out_ref[0, 1, rows, lanes] = value[1]
+                value = add_reach(table, value, lines[half])
+                out_ref[0, rows, lanes] = value[0]
+                out_ref[1, rows, lanes] = value[1]
+        write(pair).start()
 
     steps(pairs, lambda pair: column_stage(1, operand_ref.at[pair % SLOTS], weight_ref, carry_ref, grid_ref, pair), leave)
+    for pair in range(pairs):
+        write(pair).wait()
 
 
 ANY = pl.BlockSpec(memory_space=pl.ANY)
@@ -622,8 +636,8 @@
 SMEM = pl.BlockSpec(memory_space=pltpu.SMEM)
 
 
-def call(body, in_specs, out_shape, scratch=()):
-    out_specs = jax.tree.map(lambda _: VMEM, out_shape)
+def call(body, in_specs, out_shape, scratch=(), out_space=VMEM):
+    out_specs = jax.tree.map(lambda _: out_space, out_shape)
     return pl.pallas_call(
         body,
         in_specs=in_specs,
@@ -662,7 +676,8 @@
     first = call(partial(first_kernel, pairs), [VMEM] * 6, grids, passing)
     middle = [call(partial(middle_kernel, peers, section), [VMEM, VMEM], shape(peers, 8, BLOCK)) for section in range(2)]
     second = call(partial(second_kernel, pairs), [VMEM] * 9, grids, passing + small + passing[:1])
-    third = call(partial(third_kernel, pairs), [VMEM] * 6, shape(1, 2, BLOCK, width), passing + small)
+    third = call(partial(third_kernel, pairs), [VMEM] * 6, shape(1, 2, BLOCK, width),
+                 passing + small + [pltpu.VMEM((2, BLOCK, width), F32), pltpu.SemaphoreType.DMA((pairs,))], ANY)
     return prepare, first, middle, second, third
 
 

time: 74.2 us -> 73.9 us (level)
  no operation moved by 1% of the time
where the time goes in v5:
time: 73.9 us; the launch traced here: 73.6 us
  blocking collectives  46.8 us (63%)
  Pallas kernels  26.1 us (35%)
    all_to_all x2, blocking collectives, exchange(): held = lax.all_to_all(sums, 'slab', 0, 0, tiled=True)  26.2 us
    all_to_all x2, blocking collectives, exchange(): return lax.all_to_all(middle[section](held, row), 'slab', 0, 0, tiled=True)  20.6 us
    pallas_call x1, Pallas kernels, fast_shards(): second(value, back, screen, own, other, zone_ids, factor, weights, row)  11.3 us
    pallas_call x1, Pallas kernels, fast_shards(): return third(value, back, screen, factor, weights, row)  6.12 us
    pallas_call x1, Pallas kernels, fast_shards(): value, sums, screen = first(field, own, other, factor, weights, row)  5.47 us
    pallas_call x1, Pallas kernels, fast_shards(): prepare(*small, stay(fields), stay(region_ids))  2.61 us
  transfers between devices with their start and end apart: 1, of which 0 were waited for; matrix products, arithmetic and copies ran while one was open for 0% of the time, Pallas kernels for 4%

profile of v5, /device:TPU:0, one launch (start us, length us, event | category | flops | bytes accessed | tf_op | source)
XLA Modules:
  0.0 73.6 jit_solution(3389353330757269601)
XLA Ops:
  0.0 0.5 collective-permute-start
  0.5 2.6 %shard_map.73 = (bf16[2,384,768]{2,1,0:T(8,128)(2,1)S(1)}, f32[2,12,128,128]{3,2,1,0:T(8,128)S(1)}, f32[2,112,128]{2,1,0:T(8,128)S(1)}, f32[2,128,2048]{2,1,0:T(8,128)S(1)}, s32[1,128,2048]{2,1,0:T(8,128)S(1)}) custom-call(f32[2]{0:T(128)} %number_ref.1, f32[2]{0:T(128)} %length_ref.1, f32[2,16]{1,0:T(2,128)} %offset_ref.1, f32[2,32]{1,0:T(2,128)} %zone_ref.2, ...), custom_call_target="tpu_custom_call" | custom-call | tf_op jit(solution)/shard_map/pallas_call | solution.py:692
  3.1 0.0 collective-permute-done.other_ref
  3.1 0.0 copy-start
  3.1 5.5 %shard_map.74 = (f32[2,128,2048]{2,1,0:T(8,128)S(1)}, f32[16,16,128]{2,1,0:T(8,128)S(1)}, f32[2,128,2048]{2,1,0:T(8,128)S(1)}) custom-call(f32[2,128,2048]{2,1,0:T(8,128)S(1)} %get-tuple-element.16.field_ref, s32[1,128,2048]{2,1,0:T(8,128)S(1)} %get-tuple-element.17.own_ref, s32[1,128,2048]{2,1,0:T(8,128)S(1)} %collective-permute-done.other_ref, ...), custom_call_target="tpu_custom_call" | custom-call | tf_op jit(solution)/shard_map/pallas_call | solution.py:698
  8.6 15.8 %all_to_all.20.held_ref = f32[16,16,128]{2,1,0:T(8,128)S(1)} all-to-all(f32[16,16,128]{2,1,0:T(8,128)S(1)} %get-tuple-element.22), channel_id=1, replica_groups=mesh['slab'=16,'sect'=2] {'slab'}, dimensions={0} | all-to-all | bytes 262144 | tf_op jit(solution)/shard_map/all_to_all | solution.py:695
  24.3 0.3 shard_map.75
  24.7 10.5 %all_to_all.21.back_ref = f32[16,8,128]{2,1,0:T(8,128)S(1)} all-to-all(f32[16,8,128]{2,1,0:T(8,128)S(1)} %shard_map.75), channel_id=1, replica_groups=mesh['slab'=16,'sect'=2] {'slab'}, dimensions={0} | all-to-all | bytes 131072 | tf_op jit(solution)/shard_map/all_to_all | solution.py:696
  35.2 0.0 copy-done
  35.2 11.3 %shard_map.76 = (f32[2,128,2048]{2,1,0:T(8,128)S(1)}, f32[16,16,128]{2,1,0:T(8,128)S(1)}, f32[2,128,2048]{2,1,0:T(8,128)S(1)}) custom-call(f32[2,128,2048]{2,1,0:T(8,128)S(1)} %get-tuple-element.21.value_in, f32[16,8,128]{2,1,0:T(8,128)S(1)} %all_to_all.21.back_ref, f32[2,128,2048]{2,1,0:T(8,128)S(1)} %get-tuple-element.23.screen_in, ...), custom_call_target="tpu_custom_call" | custom-call | tf_op jit(solution)/shard_map/pallas_call | solution.py:700
  46.5 10.4 %all_to_all.22.held_ref = f32[16,16,128]{2,1,0:T(8,128)S(1)} all-to-all(f32[16,16,128]{2,1,0:T(8,128)S(1)} %get-tuple-element.25), channel_id=1, replica_groups=mesh['slab'=16,'sect'=2] {'slab'}, dimensions={0} | all-to-all | bytes 262144 | tf_op jit(solution)/shard_map/all_to_all | solution.py:695
  56.9 0.3 shard_map.77
  57.2 10.1 %all_to_all.23.back_ref = f32[16,8,128]{2,1,0:T(8,128)S(1)} all-to-all(f32[16,8,128]{2,1,0:T(8,128)S(1)} %shard_map.77), channel_id=1, replica_groups=mesh['slab'=16,'sect'=2] {'slab'}, dimensions={0} | all-to-all | bytes 131072 | tf_op jit(solution)/shard_map/all_to_all | solution.py:696
  67.3 6.1 %shard_map.78 = f32[1,2,128,2048]{3,2,1,0:T(8,128)} custom-call(f32[2,128,2048]{2,1,0:T(8,128)S(1)} %get-tuple-element.24.value_in, f32[16,8,128]{2,1,0:T(8,128)S(1)} %all_to_all.23.back_ref, f32[2,128,2048]{2,1,0:T(8,128)S(1)} %get-tuple-element.26.screen_in, bf16[2,384,768]{2,1,0:T(8,128)(2,1)S(1)} %get-tuple-element.18.factor_ref, ...), custom_call_target="tpu_custom_call" | custom-call | tf_op jit(solution)/shard_map/pallas_call | solution.py:702
Async XLA Ops:
  0.0 3.1 %collective-permute-start = (s32[1,128,2048]{2,1,0:T(8,128)}, s32[1,128,2048]{2,1,0:T(8,128)S(1)}, u32[]{:S(2)}, u32[]{:S(2)}) collective-permute-start(s32[1,128,2048]{2,1,0:T(8,128)} %label_any.1), channel_id=1, source_target_pairs={{0,1},{1,0},{2,3},{3,2},{4,5},{5,4},{6,7},{7,6},{8,9},{9,8},{10,11... | collective-permute-start | bytes 3145736 | tf_op jit(solution)/shard_map/ppermute | solution.py:690
  3.1 32.1 %copy-start = (s32[128,2048]{1,0:T(8,128)S(1)}, s32[128,2048]{1,0:T(8,128)}, u32[]{:S(2)}) copy-start(s32[128,2048]{1,0:T(8,128)} %zone_ref.3) | copy-start | bytes 3145732

commit v6 on v5

--- a/solution.py
+++ b/solution.py
@@ -313,10 +313,10 @@
     operand_ref[top : top + size, 384:512] = low
 
 
-def multiply(factor_ref, section, operand_ref):
+def multiply(factor_ref, section, operand_ref, count=LHS_ROWS):
     high = operand_ref[:, 0:256]
     right = jnp.concatenate([high, high, operand_ref[:, 256:512]], axis=1)
-    return lax.dot_general(factor_ref[section, 0:LHS_ROWS, :], right, (((1,), (1,)), ((), ())), preferred_element_type=F32)
+    return lax.dot_general(factor_ref[section, 0:count, :], right, (((1,), (1,)), ((), ())), preferred_element_type=F32)
 
 
 def reach_of(weight_ref, section, rows):
@@ -558,7 +558,7 @@
     scan_rows(edge_ref, carry_ref, row_ref, 0, pairs)
 
     def turn(pair):
-        out = multiply(factor_ref, 0, operand_ref.at[pair % SLOTS])
+        out = multiply(factor_ref, 0, operand_ref.at[pair % SLOTS], 2 * BLOCK)
         lines = [line_of(late_ref, 2 * pair + half) for half in range(2)]
         for top in range(0, BLOCK, CHUNK):
             rows = slice(top, top + CHUNK)
@@ -612,7 +612,7 @@
     scan_rows(edge_ref, carry_ref, row_ref, 1, pairs)
 
     def leave(pair):
-        out = multiply(factor_ref, 1, operand_ref.at[pair % SLOTS])
+        out = multiply(factor_ref, 1, operand_ref.at[pair % SLOTS], 2 * BLOCK)
         lines = [line_of(late_ref, 2 * pair + half) for half in range(2)]
         for top in range(0, BLOCK, CHUNK):
             rows = slice(top, top + CHUNK)

time: 73.9 us -> 73.8 us (level)
  no operation moved by 1% of the time
where the time goes in v6:
time: 73.8 us; the launch traced here: 73.5 us
  blocking collectives  46.8 us (63%)
  Pallas kernels  26 us (35%)
    all_to_all x2, blocking collectives, exchange(): held = lax.all_to_all(sums, 'slab', 0, 0, tiled=True)  26.2 us
    all_to_all x2, blocking collectives, exchange(): return lax.all_to_all(middle[section](held, row), 'slab', 0, 0, tiled=True)  20.6 us
    pallas_call x1, Pallas kernels, fast_shards(): second(value, back, screen, own, other, zone_ids, factor, weights, row)  11.2 us
    pallas_call x1, Pallas kernels, fast_shards(): return third(value, back, screen, factor, weights, row)  6.09 us
    pallas_call x1, Pallas kernels, fast_shards(): value, sums, screen = first(field, own, other, factor, weights, row)  5.47 us
    pallas_call x1, Pallas kernels, fast_shards(): prepare(*small, stay(fields), stay(region_ids))  2.61 us
  transfers between devices with their start and end apart: 1, of which 0 were waited for; matrix products, arithmetic and copies ran while one was open for 0% of the time, Pallas kernels for 4%

profile of v6, /device:TPU:0, one launch (start us, length us, event | category | flops | bytes accessed | tf_op | source)
XLA Modules:
  0.0 73.5 jit_solution(2387589120264267753)
XLA Ops:
  0.0 0.5 collective-permute-start
  0.5 2.6 %shard_map.73 = (bf16[2,384,768]{2,1,0:T(8,128)(2,1)S(1)}, f32[2,12,128,128]{3,2,1,0:T(8,128)S(1)}, f32[2,112,128]{2,1,0:T(8,128)S(1)}, f32[2,128,2048]{2,1,0:T(8,128)S(1)}, s32[1,128,2048]{2,1,0:T(8,128)S(1)}) custom-call(f32[2]{0:T(128)} %number_ref.1, f32[2]{0:T(128)} %length_ref.1, f32[2,16]{1,0:T(2,128)} %offset_ref.1, f32[2,32]{1,0:T(2,128)} %zone_ref.2, ...), custom_call_target="tpu_custom_call" | custom-call | tf_op jit(solution)/shard_map/pallas_call | solution.py:692
  3.1 0.0 collective-permute-done.other_ref
  3.1 0.0 copy-start
  3.1 5.5 %shard_map.74 = (f32[2,128,2048]{2,1,0:T(8,128)S(1)}, f32[16,16,128]{2,1,0:T(8,128)S(1)}, f32[2,128,2048]{2,1,0:T(8,128)S(1)}) custom-call(f32[2,128,2048]{2,1,0:T(8,128)S(1)} %get-tuple-element.16.field_ref, s32[1,128,2048]{2,1,0:T(8,128)S(1)} %get-tuple-element.17.own_ref, s32[1,128,2048]{2,1,0:T(8,128)S(1)} %collective-permute-done.other_ref, ...), custom_call_target="tpu_custom_call" | custom-call | tf_op jit(solution)/shard_map/pallas_call | solution.py:698
  8.6 15.8 %all_to_all.20.held_ref = f32[16,16,128]{2,1,0:T(8,128)S(1)} all-to-all(f32[16,16,128]{2,1,0:T(8,128)S(1)} %get-tuple-element.22), channel_id=1, replica_groups=mesh['slab'=16,'sect'=2] {'slab'}, dimensions={0} | all-to-all | bytes 262144 | tf_op jit(solution)/shard_map/all_to_all | solution.py:695
  24.3 0.3 shard_map.75
  24.7 10.5 %all_to_all.21.back_ref = f32[16,8,128]{2,1,0:T(8,128)S(1)} all-to-all(f32[16,8,128]{2,1,0:T(8,128)S(1)} %shard_map.75), channel_id=1, replica_groups=mesh['slab'=16,'sect'=2] {'slab'}, dimensions={0} | all-to-all | bytes 131072 | tf_op jit(solution)/shard_map/all_to_all | solution.py:696
  35.2 0.0 copy-done
  35.2 11.2 %shard_map.76 = (f32[2,128,2048]{2,1,0:T(8,128)S(1)}, f32[16,16,128]{2,1,0:T(8,128)S(1)}, f32[2,128,2048]{2,1,0:T(8,128)S(1)}) custom-call(f32[2,128,2048]{2,1,0:T(8,128)S(1)} %get-tuple-element.21.value_in, f32[16,8,128]{2,1,0:T(8,128)S(1)} %all_to_all.21.back_ref, f32[2,128,2048]{2,1,0:T(8,128)S(1)} %get-tuple-element.23.screen_in, ...), custom_call_target="tpu_custom_call" | custom-call | tf_op jit(solution)/shard_map/pallas_call | solution.py:700
  46.4 10.4 %all_to_all.22.held_ref = f32[16,16,128]{2,1,0:T(8,128)S(1)} all-to-all(f32[16,16,128]{2,1,0:T(8,128)S(1)} %get-tuple-element.25), channel_id=1, replica_groups=mesh['slab'=16,'sect'=2] {'slab'}, dimensions={0} | all-to-all | bytes 262144 | tf_op jit(solution)/shard_map/all_to_all | solution.py:695
  56.8 0.3 shard_map.77
  57.1 10.1 %all_to_all.23.back_ref = f32[16,8,128]{2,1,0:T(8,128)S(1)} all-to-all(f32[16,8,128]{2,1,0:T(8,128)S(1)} %shard_map.77), channel_id=1, replica_groups=mesh['slab'=16,'sect'=2] {'slab'}, dimensions={0} | all-to-all | bytes 131072 | tf_op jit(solution)/shard_map/all_to_all | solution.py:696
  67.2 6.1 %shard_map.78 = f32[1,2,128,2048]{3,2,1,0:T(8,128)} custom-call(f32[2,128,2048]{2,1,0:T(8,128)S(1)} %get-tuple-element.24.value_in, f32[16,8,128]{2,1,0:T(8,128)S(1)} %all_to_all.23.back_ref, f32[2,128,2048]{2,1,0:T(8,128)S(1)} %get-tuple-element.26.screen_in, bf16[2,384,768]{2,1,0:T(8,128)(2,1)S(1)} %get-tuple-element.18.factor_ref, ...), custom_call_target="tpu_custom_call" | custom-call | tf_op jit(solution)/shard_map/pallas_call | solution.py:702
Async XLA Ops:
  0.0 3.1 %collective-permute-start = (s32[1,128,2048]{2,1,0:T(8,128)}, s32[1,128,2048]{2,1,0:T(8,128)S(1)}, u32[]{:S(2)}, u32[]{:S(2)}) collective-permute-start(s32[1,128,2048]{2,1,0:T(8,128)} %label_any.1), channel_id=1, source_target_pairs={{0,1},{1,0},{2,3},{3,2},{4,5},{5,4},{6,7},{7,6},{8,9},{9,8},{10,11... | collective-permute-start | bytes 3145736 | tf_op jit(solution)/shard_map/ppermute | solution.py:690
  3.1 32.1 %copy-start = (s32[128,2048]{1,0:T(8,128)S(1)}, s32[128,2048]{1,0:T(8,128)}, u32[]{:S(2)}) copy-start(s32[128,2048]{1,0:T(8,128)} %zone_ref.3) | copy-start | bytes 3145732
